TPU v7x, 256 devices: a whole 4x4x8 slice. The times are simulated.
256 devices in a mesh: chan: 8 (over z_lo, core), region: 32 (over x, y, z_hi).
Axes of the slice: x: 4, y: 4, z: 8 (z_hi: 2, z_lo: 4; z = z_hi * 4 + z_lo), core: 2. Of those that a mesh axis runs over, the one named last changes fastest.
Arguments:
- latent: bfloat16 [32, 24, 24, 12, 128], P('region'), may hold values from -6 to 6
- cond_scale: float32 [128], replicated, may hold values from 0.5 to 1.5
- cond_shift: float32 [128], replicated, may hold values from -3 to 3
- fine_weight: bfloat16 [3, 3, 3, 128, 128], replicated, may hold values from -0.109375 to 0.109375
- fine_bias: float32 [128], replicated, may hold values from -3 to 3
- proj_weight: bfloat16 [8192, 1024], P(('chan', 'region')), may hold values from -0.0625 to 0.0625
- proj_bias: float32 [1024], replicated, may hold values from -3 to 3
- bottle_weight: bfloat16 [27, 1024, 1024], P(None, 'chan'), may hold values from -0.0390625 to 0.0390625
- bottle_bias: float32 [1024], replicated, may hold values from -3 to 3
- guide: float32 [1], replicated, may hold values from 1.5 to 4
Outputs:
- guided: bfloat16 [32, 6, 6, 3, 1024], P('region', None, None, None, 'chan')
All inputs are finite; a program needn't handle non-finite values.
Results may differ from a plain program's by a relative error of at most 0.012.
The roundings to bfloat16 on the way count: a program that leaves them out, or rounds other values in their place, can miss the bound.
Values may be sent and summed in bfloat16 or wider, within the bound.
A program may use at most 128 MiB of HBM per device.

v0:
```python
import jax
import jax.numpy as jnp
from jax import lax
from jax.sharding import PartitionSpec as P

FINE_WIDTH = 128
COARSE_WIDTH = 1024
TILE_SIDE = 12
STRIDE = 4
REGIONS_Y = 4
REGIONS_Z = 2


def passed_along(value, axis, steps):
    count = lax.axis_size(axis)
    leading, last = (max(0, -steps), min(count, count - steps))
    return lax.ppermute(value, axis, [(source, source + steps) for source in range(leading, last)])


def extend(block, axis_dim, stride, count):
    place = lax.axis_index("region") // stride % count
    length = block.shape[axis_dim]
    last_layer = lax.slice_in_dim(block, length - 1, length, axis=axis_dim)
    first_layer = lax.slice_in_dim(block, 0, 1, axis=axis_dim)
    arrived = [
        passed_along(layer, "region", offset)
        for layer, offset in ((last_layer, stride), (first_layer, -stride))
    ]
    below = jnp.where(place > 0, arrived[0], jnp.zeros_like(arrived[0]))
    above = jnp.where(place < count - 1, arrived[1], jnp.zeros_like(arrived[1]))
    return jnp.concatenate([below, block, above], axis=axis_dim)


def surround(block, lead):
    count_x = lax.axis_size("region") // (REGIONS_Y * REGIONS_Z)
    block = extend(block, lead + 2, 1, REGIONS_Z)
    block = extend(block, lead + 1, REGIONS_Z, REGIONS_Y)
    return extend(block, lead, REGIONS_Y * REGIONS_Z, count_x)


def fine_conv(window, weight, bias, side):
    stacked = jnp.concatenate(
        [
            window[step_x : step_x + side, step_y : step_y + side, step_z : step_z + side]
            for step_x in range(3)
            for step_y in range(3)
            for step_z in range(3)
        ],
        axis=3,
    )
    stacked = stacked.reshape(side**3, -1)
    total = jnp.dot(
        stacked, weight.reshape(-1, weight.shape[4]), preferred_element_type=jnp.float32
    )
    return jax.nn.silu(total + bias).astype(jnp.bfloat16).reshape(side, side, side, -1)


def to_patches(tile, side):
    cells = side // STRIDE
    grid = tile.reshape(cells, STRIDE, cells, STRIDE, cells, STRIDE, tile.shape[3])
    grid = grid.transpose(0, 2, 4, 6, 1, 3, 5)
    return grid.reshape(cells**3, tile.shape[3] * STRIDE**3)


def shards(
    latent,
    cond_scale,
    cond_shift,
    fine_weight,
    fine_bias,
    proj_weight,
    proj_bias,
    bottle_weight,
    bottle_bias,
    guide,
):
    side = TILE_SIDE
    cells = side // STRIDE
    channels = lax.axis_size("chan")
    chan_place = lax.axis_index("chan")
    per_copy = channels // 2
    tiles_dev = 8 // channels
    copy_index = chan_place // per_copy
    first_tile = chan_place % per_copy * tiles_dev
    width = COARSE_WIDTH // channels
    depth = FINE_WIDTH * STRIDE**3
    block = latent[0].astype(jnp.float32)
    shaped = block * cond_scale + cond_shift
    source = jnp.where(copy_index == 1, shaped, block).astype(jnp.bfloat16)
    padded = surround(source, 0)
    patches = []
    which = first_tile + 0
    window = lax.dynamic_slice(
        padded,
        (which // 2 * side, which % 2 * side, 0, 0),
        (side + 2, side + 2, side + 2, FINE_WIDTH),
    )
    patches.append(to_patches(fine_conv(window, fine_weight, fine_bias, side), side))
    patches = jnp.stack(patches)
    flat = patches.reshape(tiles_dev * cells**3, depth)
    summed = jnp.dot(
        flat,
        lax.all_gather(proj_weight, ("chan", "region"), axis=0, tiled=True),
        preferred_element_type=jnp.float32,
    )
    projected = (summed + proj_bias).astype(jnp.bfloat16)
    coarse = lax.all_to_all(projected, "chan", split_axis=1, concat_axis=0, tiled=True)
    grid = coarse.reshape(2, 2, 2, cells, cells, cells, width).transpose(0, 1, 3, 2, 4, 5, 6)
    grid = grid.reshape(2, 2 * cells, 2 * cells, cells, width)
    framed = surround(grid, 1)
    stacked = jnp.concatenate(
        [
            framed[
                :, step_x : step_x + 2 * cells, step_y : step_y + 2 * cells, step_z : step_z + cells
            ]
            for step_x in range(3)
            for step_y in range(3)
            for step_z in range(3)
        ],
        axis=4,
    )
    stacked = stacked.reshape(-1, 27 * width)
    terms = jnp.dot(
        stacked, bottle_weight.reshape(27 * width, COARSE_WIDTH), preferred_element_type=jnp.float32
    )
    summed = lax.psum_scatter(terms, "chan", scatter_dimension=1, tiled=True)
    bottle = jax.nn.silu(summed + lax.dynamic_slice_in_dim(bottle_bias, chan_place * width, width))
    bottle = bottle.reshape(2, 2 * cells, 2 * cells, cells, width)
    guided = (bottle[0] + guide[0] * (bottle[1] - bottle[0])).astype(jnp.bfloat16)
    return guided[None]


def solution(mesh):
    placed = (
        P("region", None, None, None, None),
        P(),
        P(),
        P(),
        P(),
        P(("chan", "region"), None),
        P(),
        P(None, "chan", None),
        P(),
        P(),
    )
    return jax.shard_map(
        shards,
        mesh=mesh,
        in_specs=placed,
        out_specs=P("region", None, None, None, "chan"),
        check_vma=False,
    )
```

profile of v0, /device:TPU:1, one launch (start us, length us, event | category | flops | bytes accessed | tf_op | source)
XLA Modules:
  0.0 856.9 jit_solution(12610991419264779117)
XLA Ops:
  6.5 0.7 all-gather.2.cloned.1.call-update
  7.3 2.1 fusion.1
  9.4 9.6 %collective-permute-start = (bf16[24,24,1,128]{3,1,2,0:T(8,128)(2,1)S(1)}, bf16[24,24,1,128]{3,1,2,0:T(8,128)(2,1)S(1)}, u32[]{:S(2)}, u32[]{:S(2)}) collective-permute-start(bf16[24,24,1,128]{3,1,2,0:T(8,128)(2,1)S(1)} %get-tuple-element.9), channel_id=1, source_target_pairs={{0,1},{1,2},{2,3},{3,4},{4,5},{5,6},{6,7},{7,8},{8,9},{9,10},{10,1... | collective-permute-start | bytes 442376 | tf_op jit(solution)/shard_map/ppermute | solution.py:17
  19.1 1.3 collective-permute-start.1
  20.4 1.4 collective-permute-done
  21.8 10.4 %collective-permute-done.1 = bf16[24,24,1,128]{3,1,2,0:T(8,128)(2,1)S(1)} collective-permute-done((bf16[24,24,1,128]{3,1,2,0:T(8,128)(2,1)S(1)}, bf16[24,24,1,128]{3,1,2,0:T(8,128)(2,1)S(1)}, u32[]{:S(2)}, u32[]{:S(2)}) %collective-permute-start.1) | collective-permute-done | bytes 147488 | tf_op jit(solution)/shard_map/ppermute | solution.py:17
  32.3 0.3 pad_maximum_fusion.2
  32.5 6.8 collective-permute-start.2
  39.4 1.3 collective-permute-start.3
  40.7 1.0 collective-permute-done.2
  41.9 3.7 collective-permute-done.3
  45.7 0.8 pad_maximum_fusion.4
  46.5 1.3 collective-permute-start.5
  47.9 4.2 collective-permute-start.4
  52.1 0.4 collective-permute-done.5
  52.5 1.7 collective-permute-done.4
  54.1 1.8 fusion.4
  56.1 0.2 slice_dynamic-update-slice_fusion.25
  56.4 0.2 slice_dynamic-update-slice_fusion.24
  56.6 0.3 slice_dynamic-update-slice_fusion.23
  56.9 0.3 slice_dynamic-update-slice_fusion.22
  57.3 0.3 slice_dynamic-update-slice_fusion.21
  57.6 0.3 slice_dynamic-update-slice_fusion.20
  57.9 0.3 slice_dynamic-update-slice_fusion.19
  58.3 0.3 slice_dynamic-update-slice_fusion.18
  58.6 0.2 slice_dynamic-update-slice_fusion.17
  58.9 0.2 slice_dynamic-update-slice_fusion.16
  59.4 0.3 slice_dynamic-update-slice_fusion.14
  59.7 0.3 slice_dynamic-update-slice_fusion.13
  60.0 0.3 slice_dynamic-update-slice_fusion.12
  60.4 0.3 slice_dynamic-update-slice_fusion.11
  60.7 0.3 slice_dynamic-update-slice_fusion.10
  61.0 0.3 slice_dynamic-update-slice_fusion.9
  62.1 0.3 slice_dynamic-update-slice_fusion.5
  62.4 0.3 slice_dynamic-update-slice_fusion.4
  62.7 0.3 slice_dynamic-update-slice_fusion.3
  63.1 0.3 slice_dynamic-update-slice_fusion.2
  63.4 0.3 slice_dynamic-update-slice_fusion.1
  63.7 0.3 slice_dynamic-update-slice_fusion
  64.1 9.4 %copy.70 = bf16[12,12,12,3456]{3,2,1,0:T(8,128)(2,1)} copy(bf16[12,12,12,3456]{3,1,2,0:T(8,128)(2,1)S(1)} %slice_dynamic-update-slice_fusion) | data formatting | bytes 23887872 | tf_op jit(solution)/shard_map/concatenate | solution.py:42
  73.4 18.7 %reshape.92 = bf16[1728,3456]{1,0:T(8,128)(2,1)} reshape(bf16[12,12,12,3456]{3,2,1,0:T(8,128)(2,1)} %copy.70) | data formatting | bytes 23887872 | tf_op jit(solution)/shard_map/reshape | solution.py:51
  92.1 7.7 multiply_convert_fusion
  99.8 17.5 %copy.71 = bf16[3,4,3,4,3,4,128]{5,3,1,6,4,2,0:T(4,128)(2,1)} copy(bf16[3,4,3,4,3,4,128]{6,5,4,3,2,1,0:T(4,128)(2,1)S(1)} %bitcast.33) | data formatting | bytes 884736 | tf_op jit(solution)/shard_map/reshape;reshape | solution.py:60
  117.3 37.1 %reshape_stack_reshape.3 = bf16[27,8192]{1,0:T(8,128)(2,1)S(1)} reshape(bf16[3,3,3,128,4,4,4]{6,5,4,3,2,1,0:T(4,128)(2,1)} %bitcast.24) | data formatting | bytes 884736 | tf_op jit(solution)/shard_map/reshape;stack;reshape | solution.py:100
  154.4 593.2 %all-gather.2.cloned.1.call-done = bf16[8192,1024]{1,0:T(8,128)(2,1)} async-done(((bf16[32,1024]{1,0:T(8,128)(2,1)}), bf16[8192,1024]{1,0:T(8,128)(2,1)}) %all-gather.2.cloned.1.call-update) | async-done | bytes 16777232 | tf_op jit(solution)/shard_map/all_gather | solution.py:103
  747.6 8.8 %fusion.2 = bf16[27,1024]{1,0:T(8,128)(2,1)S(1)} fusion(bf16[27,8192]{1,0:T(8,128)(2,1)S(1)} %reshape_stack_reshape.3, bf16[8192,1024]{1,0:T(8,128)(2,1)} %all-gather.2.cloned.1.call-done, f32[1024]{0:T(1024)S(1)} %copy-done.2), kind=kOutput, calls=%fused_computation.13 | convolution fusion | flops 453040128 | bytes 17278976 | tf_op jit(solution)/shard_map/dot_general | solution.py:101
  756.4 15.1 %all_to_all.16 = bf16[27,8,128]{2,0,1:T(8,128)(2,1)S(1)} all-to-all(bf16[27,8,128]{2,0,1:T(8,128)(2,1)S(1)} %copy.72), channel_id=1, replica_groups=mesh['chan'=8,'region'=32] {'chan'}, dimensions={1} | all-to-all | bytes 110592 | tf_op jit(solution)/shard_map/all_to_all | solution.py:107
  771.6 2.3 collective-permute-start.6
  773.9 1.6 collective-permute-start.7
  775.6 7.0 collective-permute-done.7
  782.7 1.3 collective-permute-start.8
  784.2 1.3 collective-permute-start.9
  785.6 3.1 collective-permute-done.9
  788.7 0.3 pad_maximum_fusion.9
  789.1 8.9 %collective-permute-start.10 = (bf16[2,1,8,5,128]{4,0,3,2,1:T(2,128)(2,1)S(1)}, bf16[2,1,8,5,128]{4,0,3,2,1:T(2,128)(2,1)S(1)}, u32[]{:S(2)}, u32[]{:S(2)}) collective-permute-start(bf16[2,1,8,5,128]{4,0,3,2,1:T(2,128)(2,1)S(1)} %get-tuple-element.32), channel_id=1, source_target_pairs={{0,8},{1,9},{2,10},{3,11},{4,12},{5,13},{6,14},{7,15},{8,16},{9,17... | collective-permute-start | bytes 61448 | tf_op jit(solution)/shard_map/ppermute | solution.py:17
  798.3 1.3 collective-permute-start.11
  800.0 2.8 collective-permute-done.11
  802.8 0.5 pad_maximum_fusion.3
  803.4 0.6 fusion.10
  806.0 5.8 fusion.16
  812.5 0.8 dynamic_slice.7
  813.2 35.1 %reduce-scatter.2.cloned.1.call-done = f32[216,128]{1,0:T(8,128)} async-done(((f32[216,1024]{1,0:T(8,128)}), f32[216,128]{1,0:T(8,128)}) %reduce-scatter.2.cloned.1.call-update) | async-done | bytes 110608 | tf_op jit(solution)/shard_map/reduce_scatter | solution.py:126
  848.4 0.9 divide_multiply_fusion
  849.4 0.6 add_convert_fusion
  (126 shorter events, 4.8 us)
Async XLA Ops:
  6.5 85.6 %copy-start = (bf16[3,3,3,128,128]{4,3,2,1,0:T(8,128)(2,1)S(1)}, bf16[3,3,3,128,128]{4,3,2,1,0:T(8,128)(2,1)}, u32[]{:S(2)}) copy-start(bf16[3,3,3,128,128]{4,3,2,1,0:T(8,128)(2,1)} %param.13) | copy-start | bytes 2654212
  6.5 741.0 %all-gather.2.cloned.1.call-start = ((), (), s32[]{:S(2)}) async-start(), calls=%async_computation.2 | async-start | bytes 16842752 | tf_op jit(solution)/shard_map/all_gather | solution.py:103
  7.3 841.1 %reduce-scatter.2.cloned.1.call-start = ((), (), s32[]{:S(2)}) async-start(), calls=%async_computation.3 | async-start | bytes 995328 | tf_op jit(solution)/shard_map/reduce_scatter | solution.py:126
  9.4 12.4 %collective-permute-start = (bf16[24,24,1,128]{3,1,2,0:T(8,128)(2,1)S(1)}, bf16[24,24,1,128]{3,1,2,0:T(8,128)(2,1)S(1)}, u32[]{:S(2)}, u32[]{:S(2)}) collective-permute-start(bf16[24,24,1,128]{3,1,2,0:T(8,128)(2,1)S(1)} %get-tuple-element.9), channel_id=1, source_target_pairs={{0,1},{1,2},{2,3},{3,4},{4,5},{5,6},{6,7},{7,8},{8,9},{9,10},{10,1... | collective-permute-start | bytes 442376 | tf_op jit(solution)/shard_map/ppermute | solution.py:17
  19.1 13.2 %collective-permute-start.1 = (bf16[24,24,1,128]{3,1,2,0:T(8,128)(2,1)S(1)}, bf16[24,24,1,128]{3,1,2,0:T(8,128)(2,1)S(1)}, u32[]{:S(2)}, u32[]{:S(2)}) collective-permute-start(bf16[24,24,1,128]{3,1,2,0:T(8,128)(2,1)S(1)} %get-tuple-element.10), channel_id=1, source_target_pairs={{1,0},{2,1},{3,2},{4,3},{5,4},{6,5},{7,6},{8,7},{9,8},{10,9},{11,1... | collective-permute-start | bytes 442376 | tf_op jit(solution)/shard_map/ppermute | solution.py:17
  32.5 9.2 %collective-permute-start.2 = (bf16[24,1,14,128]{3,1,2,0:T(2,128)(2,1)S(1)}, bf16[24,1,14,128]{3,1,2,0:T(2,128)(2,1)S(1)}, u32[]{:S(2)}, u32[]{:S(2)}) collective-permute-start(bf16[24,1,14,128]{3,1,2,0:T(2,128)(2,1)S(1)} %get-tuple-element.7), channel_id=1, source_target_pairs={{0,2},{1,3},{2,4},{3,5},{4,6},{5,7},{6,8},{7,9},{8,10},{9,11},{10,... | collective-permute-start | bytes 258056 | tf_op jit(solution)/shard_map/ppermute | solution.py:17
  39.4 6.2 collective-permute-start.3
  46.5 5.9 collective-permute-start.5
  47.9 6.2 collective-permute-start.4
  73.4 18.7 %copy-start.3 = (f32[128]{0:T(128)S(1)}, f32[128]{0:T(128)}, u32[]{:S(2)}) copy-start(f32[128]{0:T(128)} %param.14) | copy-start | bytes 1540
  117.3 630.3 %copy-start.2 = (f32[1024]{0:T(1024)S(1)}, f32[1024]{0:T(1024)}, u32[]{:S(2)}) copy-start(f32[1024]{0:T(1024)} %param.16) | copy-start | bytes 12292
  771.6 3.9 collective-permute-start.6
  773.9 8.7 %collective-permute-start.7 = (bf16[2,6,6,1,128]{4,0,3,2,1:T(2,128)(2,1)S(1)}, bf16[2,6,6,1,128]{4,0,3,2,1:T(2,128)(2,1)S(1)}, u32[]{:S(2)}, u32[]{:S(2)}) collective-permute-start(bf16[2,6,6,1,128]{4,0,3,2,1:T(2,128)(2,1)S(1)} %get-tuple-element.48), channel_id=1, source_target_pairs={{1,0},{2,1},{3,2},{4,3},{5,4},{6,5},{7,6},{8,7},{9,8},{10,9},{11,1... | collective-permute-start | bytes 55304 | tf_op jit(solution)/shard_map/ppermute | solution.py:17
  782.7 2.9 collective-permute-start.8
  784.2 4.5 collective-permute-start.9
  789.1 10.9 %collective-permute-start.10 = (bf16[2,1,8,5,128]{4,0,3,2,1:T(2,128)(2,1)S(1)}, bf16[2,1,8,5,128]{4,0,3,2,1:T(2,128)(2,1)S(1)}, u32[]{:S(2)}, u32[]{:S(2)}) collective-permute-start(bf16[2,1,8,5,128]{4,0,3,2,1:T(2,128)(2,1)S(1)} %get-tuple-element.32), channel_id=1, source_target_pairs={{0,8},{1,9},{2,10},{3,11},{4,12},{5,13},{6,14},{7,15},{8,16},{9,17... | collective-permute-start | bytes 61448 | tf_op jit(solution)/shard_map/ppermute | solution.py:17
  798.3 4.5 collective-permute-start.11
  806.0 44.0 %copy-start.1 = (bf16[3,3,3,128,128]{4,3,2,1,0:T(8,128)(2,1)S(1)}, bf16[3,3,3,128,128]{4,3,2,1,0:T(8,128)(2,1)}, u32[]{:S(2)}) copy-start(bf16[3,3,3,128,128]{4,3,2,1,0:T(8,128)(2,1)} %param.13) | copy-start | bytes 2654212
Sparse Core Ops, SparseCore 0:
  9.2 738.3 all-gather.1
  811.9 36.3 reduce-scatter.1
where the time goes:
time: 860 us; the launch traced here: 857 us
  waiting for transfers between devices  660 us (77%)
  local copies, waits for them, and re-layouts  94.6 us (11%)
  starting transfers between devices  41.1 us (5%)
  matrix products  22.2 us (3%)
  between operations  15.2 us (2%)
  blocking collectives  15.1 us (2%)
    all_gather x1, waiting for transfers between devices, shards(): lax.all_gather(proj_weight, ('chan', 'region'), axis=0, tiled=True)  593 us
    ppermute x12, starting transfers between devices, passed_along(): lax.ppermute(value, axis, [(source, source + steps) for source in range(l...  41.1 us
    another operation x1, local copies, waits for them, and re-layouts, shards(): flat = patches.reshape(tiles_dev * cells ** 3, depth)  37.1 us
    reduce_scatter x1, waiting for transfers between devices, shards(): summed = lax.psum_scatter(terms, 'chan', scatter_dimension=1, tiled=True)  35.1 us
    ppermute x12, waiting for transfers between devices, passed_along(): lax.ppermute(value, axis, [(source, source + steps) for source in range(l...  31.4 us
    reshape x1, local copies, waits for them, and re-layouts, fine_conv(): stacked = stacked.reshape(side ** 3, -1)  18.7 us
    another operation x1, local copies, waits for them, and re-layouts, to_patches(): tile.reshape(cells, STRIDE, cells, STRIDE, cells, STRIDE, tile.shape[3])  17.5 us
  transfers between devices with their start and end apart: 14, of which 11 were waited for; matrix products, arithmetic and copies ran while one was open for 12% of the time, Pallas kernels for 0%

commit v1 on v0

v1 whole, which is shorter than its diff:
```python
import functools

import jax
import jax.numpy as jnp
from jax import lax
from jax.experimental import pallas as pl
from jax.experimental.pallas import tpu as pltpu
from jax.sharding import PartitionSpec as P

F32 = jnp.float32
BF16 = jnp.bfloat16
SIDES = (-1, 1)


def place_of():
    c = lax.axis_index("chan")
    r = lax.axis_index("region")
    return c // 2, c % 2, r // 8, r // 2 % 4, r % 2


def device_at(zlo, core, x, y, zhi):
    return (zlo * 2 + core, (x * 4 + y) * 2 + zhi)


class Mail:
    def __init__(self, send, recv):
        self.send, self.recv, self.used = send, recv, 0
        self.all = []

    def post(self, src, dst, target):
        copy = pltpu.make_async_remote_copy(
            src_ref=src,
            dst_ref=dst,
            send_sem=self.send.at[self.used],
            recv_sem=self.recv.at[self.used],
            device_id=target,
            device_id_type=pl.DeviceIdType.MESH,
        )
        self.used += 1
        copy.start()
        self.all.append(copy)
        return copy


def silu(v):
    return v / (1.0 + jnp.exp(-v))


def kernel(
    lat, scale, shift, fw, fbias, pw, pbias, bw, bbias, guide,
    out,
    L, G, A, FW, WZ, H, HID, WR, WP, PM, BW, CF, FR, FB, T, TS, RB, YB,
    HX, HY, HC, ZS, ZSY, ZP, ZX, ZY, ZC,
    CX, CY, CC, CZ, CZX, CZY, CZC,
    lsem, ssem, rsem,
):
    zlo, core, x, y, zhi = place_of()
    mail = Mail(ssem, rsem)

    def near(sx, sy, sz):
        return device_at(zlo, core, (x + sx) % 4, (y + sy) % 4, (zhi + sz) % 2)

    def line(dz):
        z = (zhi * 4 + zlo + dz) % 8
        return device_at(z % 4, core, x, y, z // 4)

    partner = device_at(zlo, 1 - core, x, y, zhi)

    loads = []

    def load(src, dst):
        copy = pltpu.make_async_copy(src, dst, lsem.at[len(loads)])
        copy.start()
        loads.append(copy)
        return copy

    load_lat = load(lat.at[0], L)
    load_fw = load(fw, FW)
    me_ch = lambda: (core, x, y)
    own_w = load(
        pw.at[:, pl.ds(pl.multiple_of(zlo * 256, 256), 256)],
        WR.at[zlo, core, x, y, pl.ds(pl.multiple_of(zhi * 32, 32), 32)],
    )
    own_b = [
        load(
            bw.at[:, :, pl.ds(pl.multiple_of((2 * z + core) * 128, 128), 128)],
            BW.at[:, pl.ds(pl.multiple_of(core * 128, 128), 128), z * 128 : z * 128 + 128],
        )
        for z in range(4)
    ]

    barrier = pltpu.get_barrier_semaphore()
    friends = [near(sx, sy, 0) for sx in (-1, 0, 1) for sy in (-1, 0, 1) if sx or sy]
    friends += [near(sx, sy, 1) for sx in (-1, 0, 1) for sy in (-1, 0, 1)]
    friends += [near(2, 0, 0), near(0, 2, 0)]
    friends += [line(d) for d in (1, 2, 3, 5, 6, 7)]
    friends += [partner]
    for friend in friends:
        pl.semaphore_signal(barrier, inc=1, device_id=friend, device_id_type=pl.DeviceIdType.MESH)
    pl.semaphore_wait(barrier, len(friends))

    edge = {-1: 23, 1: 0}
    slot = {-1: 0, 1: 1}
    fine = []
    for s in SIDES:
        fine.append(mail.post(lat.at[0, edge[s]], HX.at[slot[s]], near(-s, 0, 0)))
        fine.append(mail.post(lat.at[0, :, edge[s]], HY.at[slot[s]], near(0, -s, 0)))
    for sx in SIDES:
        for sy in SIDES:
            fine.append(
                mail.post(
                    lat.at[0, edge[sx], edge[sy]],
                    HC.at[slot[sx] * 2 + slot[sy]],
                    near(-sx, -sy, 0),
                )
            )

    rows_here = pl.ds(pl.multiple_of(zhi * 32, 32), 32)
    first = []
    for d in (4, 3, 5, 2, 6, 1, 7):
        target = line(d)
        z_there = (zhi * 4 + zlo + d) % 8 % 4
        first.append(
            mail.post(
                pw.at[:, pl.ds(pl.multiple_of(z_there * 256, 256), 256)],
                WR.at[zlo, core, x, y, rows_here],
                target,
            )
        )

    load_lat.wait()

    def widen(i, carry):
        for j in range(24):
            G[pl.ds((i + 1) * 416 + (j + 1) * 16 + 1, 12), :] = L[i, j].astype(F32)
        return carry

    lax.fori_loop(0, 24, widen, 0)

    def edge_rows(start, stride):
        low = G[pl.ds(start + 1, 24, stride=stride), :]
        high = G[pl.ds(start + 12, 24, stride=stride), :]
        return jnp.where(zhi == 0, high, low).astype(BF16)

    def plane(i, carry):
        ZS[i] = edge_rows((i + 1) * 416 + 16, 16)
        return carry

    lax.fori_loop(0, 24, plane, 0)
    ZSY[0] = edge_rows(416 + 16, 416)
    ZSY[1] = edge_rows(416 + 24 * 16, 416)

    half = pl.ds(pl.multiple_of(core * 12, 12), 12)
    face = mail.post(ZS.at[half], ZP.at[half], near(0, 0, 1))
    above = []
    strip = {-1: 1, 1: 0}
    for s in SIDES:
        above.append(mail.post(ZS.at[edge[s]], ZX.at[slot[s]], near(-s, 0, 1)))
        above.append(mail.post(ZSY.at[strip[s]], ZY.at[slot[s]], near(0, -s, 1)))
    for sx in SIDES:
        for sy in SIDES:
            above.append(
                mail.post(
                    ZSY.at[strip[sy]], ZC.at[slot[sx] * 2 + slot[sy]], near(-sx, -sy, 1)
                )
            )

    swap_b = [
        mail.post(
            bw.at[:, :, pl.ds(pl.multiple_of((2 * z + 1 - core) * 128, 128), 128)],
            BW.at[:, pl.ds(pl.multiple_of(core * 128, 128), 128), z * 128 : z * 128 + 128],
            partner,
        )
        for z in range(4)
    ]

    load_fw.wait()
    for dx in range(3):
        for dz in range(3):
            for step in range(4):
                for o in range(2):
                    dy = step - o
                    here = (dx * 3 + dz, slice(step * 128, step * 128 + 128), slice(o * 128, o * 128 + 128))
                    if 0 <= dy < 3:
                        WZ[here] = FW[dx, dy, dz]
                    else:
                        WZ[here] = jnp.zeros((128, 128), BF16)
    row = lax.broadcasted_iota(jnp.int32, (256, 256), 0)
    col = lax.broadcasted_iota(jnp.int32, (256, 256), 1)
    PM[...] = jnp.where(col == (row & 15) * 16 + (row >> 4), 1.0, 0.0).astype(BF16)
    H[:, 384:416, :] = jnp.zeros((4, 32, 128), F32)

    own_w.wait()
    for copy in first:
        copy.wait_recv()
    second = []
    for d in (2, 1, 3):
        second.append(
            mail.post(WR.at[0:2, core, x, y], WR.at[0:2, core, x, y], near(d, 0, 0))
        )
        second.append(
            mail.post(WR.at[2:4, core, x, y], WR.at[2:4, core, x, y], near(0, d, 0))
        )

    for copy in fine:
        copy.wait_recv()

    def border(j, carry):
        for s in (0, 1):
            at = s * 25
            G[pl.ds(at * 416 + (j + 1) * 16 + 1, 12), :] = HX[s, j].astype(F32)
            G[pl.ds((j + 1) * 416 + at * 16 + 1, 12), :] = HY[s, j].astype(F32)
        return carry

    lax.fori_loop(0, 24, border, 0)
    for sx in (0, 1):
        for sy in (0, 1):
            G[sx * 25 * 416 + sy * 25 * 16 + 1 : sx * 25 * 416 + sy * 25 * 16 + 13, :] = HC[
                sx * 2 + sy
            ].astype(F32)

    face.wait_recv()
    relay = mail.post(ZP.at[half], ZP.at[half], partner)
    for copy in above:
        copy.wait_recv()

    for copy in second:
        copy.wait_recv()
    third = []
    for d in (2, 1, 3):
        third.append(
            mail.post(WR.at[0:2, core, :, y], WR.at[0:2, core, :, y], near(0, d, 0))
        )
        third.append(
            mail.post(WR.at[2:4, core, x], WR.at[2:4, core, x], near(d, 0, 0))
        )
    hand = [
        mail.post(WR.at[0:2, core, :, y], WR.at[0:2, core, :, y], partner),
        mail.post(WR.at[2:4, core, x], WR.at[2:4, core, x], partner),
    ]

    zrow = 13 - 13 * zhi
    relay.wait_recv()

    def cap(i, carry):
        G[pl.ds((i + 1) * 416 + 16 + zrow, 24, stride=16), :] = ZP[i].astype(F32)
        return carry

    lax.fori_loop(0, 24, cap, 0)
    for s in (0, 1):
        G[pl.ds(s * 25 * 416 + 16 + zrow, 24, stride=16), :] = ZX[s].astype(F32)
        G[pl.ds(416 + s * 25 * 16 + zrow, 24, stride=416), :] = ZY[s].astype(F32)
    for sx in (0, 1):
        for sy in (0, 1):
            strip_rows = ZC[sx * 2 + sy].astype(F32)
            pick = 0 if sx else 23
            G[pl.ds(sx * 25 * 416 + sy * 25 * 16 + zrow, 1), :] = strip_rows[pick : pick + 1]

    second_copy = core == 1
    gain = jnp.where(second_copy, scale[...], 1.0)
    offset = jnp.where(second_copy, shift[...], 0.0)
    level = lax.broadcasted_iota(jnp.int32, (16, 128), 0)

    def fill(i, carry):
        inside = (i > 0) | (x > 0)
        inside = inside & ((i < 25) | (x < 3))
        for j in range(26):
            ok = inside
            if j == 0:
                ok = ok & (y > 0)
            if j == 25:
                ok = ok & (y < 3)
            lowest = jnp.where(ok, 1 - zhi, 100)
            w = G[pl.ds(pl.multiple_of(i * 416 + j * 16, 16), 16), :] * gain + offset
            w = jnp.where((level >= lowest) & (level <= 13 - zhi), w, 0.0)
            at = pl.ds(pl.multiple_of(i * 16, 16), 16)
            lanes = slice(j * 128, j * 128 + 128)
            A[0, at, lanes] = w.astype(BF16)
            A[1, at, lanes] = pltpu.roll(w, 15, 0).astype(BF16)
            A[2, at, lanes] = pltpu.roll(w, 14, 0).astype(BF16)
        return carry

    lax.fori_loop(0, 26, fill, 0)

    bias = jnp.concatenate([fbias[...], fbias[...]], axis=1)

    def conv(cy, carry):
        for pair in range(2):
            start = pl.multiple_of((cy * 4 + pair * 2) * 128, 256)
            total = None
            for dx in range(3):
                for dz in range(3):
                    term = jnp.dot(
                        A[dz, dx * 16 : dx * 16 + 384, pl.ds(start, 512)],
                        WZ[dx * 3 + dz],
                        preferred_element_type=F32,
                    )
                    total = term if total is None else total + term
            value = silu(total + bias)
            for i in range(24):
                at = (i % 4 * 6 + i // 4) * 16
                for o in range(2):
                    H[pair * 2 + o, at : at + 16, :] = value[
                        i * 16 : i * 16 + 16, o * 128 : o * 128 + 128
                    ]
        for yo in range(4):
            for xo in range(4):
                for zo in range(4):
                    part = xo * 16 + yo * 4 + zo
                    HID[pl.ds(pl.multiple_of(cy * 32, 32), 32), part * 128 : part * 128 + 128] = H[
                        yo, pl.ds(xo * 96 + zo, 32, stride=4), :
                    ].astype(BF16)
        return carry

    lax.fori_loop(0, 6, conv, 0)

    for n, d in enumerate((2, 1, 3)):
        third[2 * n].wait_recv()
        y_from = (y + 4 - d) % 4
        hand.append(mail.post(WR.at[0:2, core, :, y_from], WR.at[0:2, core, :, y_from], partner))
        third[2 * n + 1].wait_recv()
        x_from = (x + 4 - d) % 4
        hand.append(mail.post(WR.at[2:4, core, x_from], WR.at[2:4, core, x_from], partner))
    for copy in hand:
        copy.wait_recv()

    def regroup(i, carry):
        z = i // 8
        k = i // 4 % 2
        block = pl.ds(pl.multiple_of(i % 4 * 16, 16), 16)
        rows = WR[z, k, :, :, block, :].reshape(256, 256)
        turned = jnp.dot(PM[...], rows, preferred_element_type=F32).astype(BF16)
        WP[block, pl.ds(pl.multiple_of((z * 2 + k) * 16, 16), 16), :] = turned.reshape(16, 16, 256)
        return carry

    lax.fori_loop(0, 32, regroup, 0)

    def project(i, total):
        lanes = pl.ds(pl.multiple_of(i * 1024, 1024), 1024)
        rows = WP[pl.ds(i * 8, 8)].reshape(1024, 256)
        return total + jnp.dot(HID[:, lanes], rows, preferred_element_type=F32)

    total = lax.fori_loop(0, 8, project, jnp.zeros((192, 256), F32))
    total = total + pbias[:, pl.ds(pl.multiple_of(zlo * 256, 256), 256)]
    total = total.astype(BF16).astype(F32)
    for h in range(2):
        CF[h] = total[:, h * 128 : h * 128 + 128]

    mine = FR.at[core]
    for cz in range(3):
        for cx in range(6):
            for h in range(2):
                mine[h, cz + 1, (cx + 1) * 8 + 1 : (cx + 1) * 8 + 7, :] = CF[
                    h, pl.ds(cx * 4 + cz, 6, stride=32), :
                ]
    for cz in range(3):
        for h in range(2):
            YB[0, h, cz] = mine[h, cz + 1, pl.ds(1, 8, stride=8), :]
            YB[1, h, cz] = mine[h, cz + 1, pl.ds(6, 8, stride=8), :]
    top = 2 - 2 * zhi
    wide = {-1: 6, 1: 1}
    around = []
    around.append(mail.post(mine.at[:, top + 1, 8:56], CZ, near(0, 0, 1)))
    for sx in SIDES:
        for sy in SIDES:
            around.append(
                mail.post(YB.at[strip[sy], :, top], CZC.at[slot[sx] * 2 + slot[sy]], near(-sx, -sy, 1))
            )
    for s in SIDES:
        column = slice(wide[s] * 8, wide[s] * 8 + 8)
        around.append(mail.post(mine.at[:, top + 1, column], CZX.at[slot[s]], near(-s, 0, 1)))
        around.append(mail.post(YB.at[strip[s], :, top], CZY.at[slot[s]], near(0, -s, 1)))
    for sx in SIDES:
        for sy in SIDES:
            around.append(
                mail.post(YB.at[strip[sy]], CC.at[slot[sx] * 2 + slot[sy]], near(-sx, -sy, 0))
            )
    for s in SIDES:
        column = slice(wide[s] * 8, wide[s] * 8 + 8)
        around.append(mail.post(mine.at[:, 1:4, column], CX.at[slot[s]], near(-s, 0, 0)))
        around.append(mail.post(YB.at[strip[s]], CY.at[slot[s]], near(0, -s, 0)))
    for copy in around:
        copy.wait_send()
    for copy in around:
        copy.wait_recv()

    place8 = lax.broadcasted_iota(jnp.int32, (8, 128), 0)
    x_ok = (x > 0, x < 3)
    y_ok = (y > 0, y < 3)

    def frame(h, cz, in_x, in_y, in_corner):
        for s in (0, 1):
            mine[h, cz, s * 56 : s * 56 + 8, :] = jnp.where(x_ok[s], in_x[s], 0.0)
        for s in (0, 1):
            low = jnp.broadcast_to(in_corner[s][6:7], (8, 128))
            high = jnp.broadcast_to(in_corner[2 + s][1:2], (8, 128))
            value = jnp.where(place8 == 0, jnp.where(x_ok[0], low, 0.0), in_y[s])
            value = jnp.where(place8 == 7, jnp.where(x_ok[1], high, 0.0), value)
            mine[h, cz, pl.ds(s * 7, 8, stride=8), :] = jnp.where(y_ok[s], value, 0.0)

    lid = 4 - 4 * zhi
    for h in range(2):
        for cz in range(3):
            frame(
                h,
                cz + 1,
                [CX[s, h, cz] for s in (0, 1)],
                [CY[s, h, cz] for s in (0, 1)],
                [CC[s, h, cz] for s in range(4)],
            )
        mine[h, 4 * zhi] = jnp.zeros((64, 128), F32)
        mine[h, lid, 8:56, :] = CZ[h]
        frame(
            h,
            lid,
            [CZX[s, h] for s in (0, 1)],
            [CZY[s, h] for s in (0, 1)],
            [CZC[s, h] for s in range(4)],
        )

    trade = mail.post(FR.at[core], FR.at[core], partner)
    trade.wait_recv()

    def stack(i, carry):
        c = i // 5
        z = i % 5
        for h in range(2):
            w = FR[c, h, z]
            for dy in range(3):
                turned = w if dy == 0 else pltpu.roll(w, 64 - dy, 0)
                for dx in range(3):
                    FB[dx * 3 + dy, c, z, :, h * 128 : h * 128 + 128] = turned[
                        dx * 8 : dx * 8 + 48
                    ].astype(BF16)
        return carry

    lax.fori_loop(0, 10, stack, 0)

    for copy in own_b:
        copy.wait()
    for copy in swap_b:
        copy.wait_recv()
    T[...] = jnp.zeros((288, 512), F32)

    def bottle(i, carry):
        total = T[...]
        for dz in range(3):
            rows = FB[i, :, dz : dz + 3].reshape(288, 256)
            total = total + jnp.dot(rows, BW[i * 3 + dz], preferred_element_type=F32)
        T[...] = total
        return carry

    lax.fori_loop(0, 9, bottle, 0)

    for c in range(2):
        for g in range(18):
            at = (c * 18 + g) * 8
            for z in range(4):
                TS[z, c, g * 6 : g * 6 + 6, :] = T[at : at + 6, z * 128 : z * 128 + 128]

    gather = []
    for d in (2, 1, 3):
        z = (zlo + d) % 4
        gather.append(mail.post(TS.at[z], RB.at[d - 1], device_at(z, core, x, y, zhi)))
    for copy in gather:
        copy.wait_recv()
    lane = pl.ds(pl.multiple_of((zlo * 2 + core) * 128, 128), 128)
    result = []
    for c in range(2):
        value = TS[zlo, c] + RB[0, c] + RB[1, c] + RB[2, c]
        result.append(silu(value + bbias[:, lane]))
    out[...] = (result[0] + guide[0] * (result[1] - result[0])).astype(BF16)

    for copy in mail.all:
        if not any(copy is other for other in around):
            copy.wait_send()


MESSAGES = 80


def shards(lat, scale, shift, fw, fbias, pw, pbias, bw, bbias, guide):
    anywhere = pl.BlockSpec(memory_space=pl.ANY)
    vmem = pl.BlockSpec(memory_space=pltpu.VMEM)
    scratch = [
        pltpu.VMEM((24, 24, 12, 128), BF16),
        pltpu.VMEM((26 * 416, 128), F32),
        pltpu.VMEM((3, 416, 26 * 128), BF16),
        pltpu.VMEM((3, 3, 3, 128, 128), BF16),
        pltpu.VMEM((9, 512, 256), BF16),
        pltpu.VMEM((4, 416, 128), F32),
        pltpu.VMEM((192, 8192), BF16),
        pltpu.VMEM((4, 2, 4, 4, 64, 256), BF16),
        pltpu.VMEM((64, 128, 256), BF16),
        pltpu.VMEM((256, 256), BF16),
        pltpu.VMEM((27, 256, 512), BF16),
        pltpu.VMEM((2, 192, 128), F32),
        pltpu.VMEM((2, 2, 5, 64, 128), F32),
        pltpu.VMEM((9, 2, 5, 48, 256), BF16),
        pltpu.VMEM((288, 512), F32),
        pltpu.VMEM((4, 2, 108, 128), F32),
        pltpu.VMEM((3, 2, 108, 128), F32),
        pltpu.VMEM((2, 2, 3, 8, 128), F32),
        pltpu.VMEM((2, 24, 12, 128), BF16),
        pltpu.VMEM((2, 24, 12, 128), BF16),
        pltpu.VMEM((4, 12, 128), BF16),
        pltpu.VMEM((24, 24, 128), BF16),
        pltpu.VMEM((2, 24, 128), BF16),
        pltpu.VMEM((24, 24, 128), BF16),
        pltpu.VMEM((2, 24, 128), BF16),
        pltpu.VMEM((2, 24, 128), BF16),
        pltpu.VMEM((4, 24, 128), BF16),
        pltpu.VMEM((2, 2, 3, 8, 128), F32),
        pltpu.VMEM((2, 2, 3, 8, 128), F32),
        pltpu.VMEM((4, 2, 3, 8, 128), F32),
        pltpu.VMEM((2, 48, 128), F32),
        pltpu.VMEM((2, 2, 8, 128), F32),
        pltpu.VMEM((2, 2, 8, 128), F32),
        pltpu.VMEM((4, 2, 8, 128), F32),
        pltpu.SemaphoreType.DMA((8,)),
        pltpu.SemaphoreType.DMA((MESSAGES,)),
        pltpu.SemaphoreType.DMA((MESSAGES,)),
    ]
    rows = pl.pallas_call(
        kernel,
        out_shape=jax.ShapeDtypeStruct((108, 128), BF16),
        in_specs=[
            anywhere, vmem, vmem, anywhere, vmem, anywhere, vmem, anywhere, vmem,
            pl.BlockSpec(memory_space=pltpu.SMEM),
        ],
        out_specs=vmem,
        scratch_shapes=scratch,
        compiler_params=pltpu.CompilerParams(
            collective_id=0, has_side_effects=True, vmem_limit_bytes=67043328
        ),
        name="denoise",
    )(
        lat,
        scale.reshape(1, -1),
        shift.reshape(1, -1),
        fw,
        fbias.reshape(1, -1),
        pw,
        pbias.reshape(1, -1),
        bw,
        bbias.reshape(1, -1),
        guide,
    )
    return rows.reshape(3, 6, 6, 128).transpose(1, 2, 0, 3)[None]


def solution(mesh):
    placed = (
        P("region", None, None, None, None),
        P(),
        P(),
        P(),
        P(),
        P(("chan", "region"), None),
        P(),
        P(None, "chan", None),
        P(),
        P(),
    )
    return jax.shard_map(
        shards,
        mesh=mesh,
        in_specs=placed,
        out_specs=P("region", None, None, None, "chan"),
        check_vma=False,
    )
```

time: 860 us -> 83.9 us (0.10)
  waiting for transfers between devices: 660 us -> 0 us
  local copies, waits for them, and re-layouts: 94.6 us -> 4.85 us
  Pallas kernels: 0 us -> 77.9 us
  starting transfers between devices: 41.1 us -> 0 us
  matrix products: 22.2 us -> 0 us
  blocking collectives: 15.1 us -> 0 us
  between operations: 15.2 us -> 0.66 us
    all_gather x1 -> x0, waiting for transfers between devices: 593 us -> none  [shards(): lax.all_gather(proj_weight, ('chan', 'region'), axis=0, tiled=True)]
    pallas_call x0 -> x1, Pallas kernels: none -> 77.9 us  [shards(): pl.pallas_call(kernel, out_shape=jax.ShapeDtypeStruct((108, 128), BF16),...]
    another operation x2 -> x0, local copies, waits for them, and re-layouts: 54.6 us -> none  [the longest x1 37.1 us: shards(): flat = patches.reshape(tiles_dev * cells ** 3, depth)]
    ppermute x12 -> x0, starting transfers between devices: 41.1 us -> none  [passed_along(): lax.ppermute(value, axis, [(source, source + steps) for source in range(l...]
    reduce_scatter x1 -> x0, waiting for transfers between devices: 35.1 us -> none  [shards(): summed = lax.psum_scatter(terms, 'chan', scatter_dimension=1, tiled=True)]
    ppermute x12 -> x0, waiting for transfers between devices: 31.4 us -> none  [passed_along(): lax.ppermute(value, axis, [(source, source + steps) for source in range(l...]
    dot_general x3 -> x0, matrix products: 22.2 us -> none  [the longest x1 8.75 us: shards(): jnp.dot(flat, lax.all_gather(proj_weight, ('chan', 'region'), axis=0, til...]
    reshape x1 -> x2, local copies, waits for them, and re-layouts: 18.7 us -> 1.39 us  [shards(): return rows.reshape(3, 6, 6, 128).transpose(1, 2, 0, 3)[None]]
  transfers between devices with their start and end apart: 14 -> 0, of which waited for: 11 -> 0; matrix products, arithmetic and copies ran while one was open for 12% -> 0% of each run, Pallas kernels for 0% -> 0%
where the time goes in v1:
time: 83.9 us; the launch traced here: 83.4 us
  Pallas kernels  77.9 us (93%)
  local copies, waits for them, and re-layouts  4.85 us (6%)
    pallas_call x1, Pallas kernels, shards(): pl.pallas_call(kernel, out_shape=jax.ShapeDtypeStruct((108, 128), BF16),...  77.9 us
    unnamed x1, local copies, waits for them, and re-layouts  3.45 us

profile of v1, /device:TPU:1, one launch (start us, length us, event | category | flops | bytes accessed | tf_op | source)
XLA Modules:
  0.0 83.4 jit_solution(6837023131681021994)
XLA Ops:
  0.7 3.5 %copy.11.lat = bf16[1,24,24,12,128]{4,3,2,1,0:T(8,128)(2,1)} copy(bf16[1,24,24,12,128]{4,2,3,1,0:T(8,128)(2,1)} %param.10) | data formatting | bytes 3538944 | tf_op args[0]
  4.1 77.9 %denoise.1 = bf16[108,128]{1,0:T(8,128)(2,1)} custom-call(bf16[1,24,24,12,128]{4,3,2,1,0:T(8,128)(2,1)} %copy.11.lat, f32[1,128]{1,0:T(1,128)} %bitcast.12, f32[1,128]{1,0:T(1,128)} %bitcast.13, bf16[3,3,3,128,128]{4,3,2,1,0:T(8,128)(2,1)} %fw.1, f32[1,128]{1,0:T(1,128)} %bitcast.14, bf16[32,1024]{1,0:T(8,128)(2,1)} %pw.1, f32[1,1024]{1,0:T(1,128)} %bitcast.10, ...), custom_call_target="tpu_custom_call" | custom-call | tf_op jit(solution)/shard_map/denoise/pallas_call | solution.py:524
  82.0 0.8 reshape.23
  82.8 0.6 copy.14

commit v2 on v0

v2 whole, which is shorter than its diff:
```python
import functools

import jax
import jax.numpy as jnp
from jax import lax
from jax.experimental import pallas as pl
from jax.experimental.pallas import tpu as pltpu
from jax.sharding import PartitionSpec as P

F32 = jnp.float32
BF16 = jnp.bfloat16
SIDES = (-1, 1)


def place_of():
    c = lax.axis_index("chan")
    r = lax.axis_index("region")
    return c // 2, c % 2, r // 8, r // 2 % 4, r % 2


def device_at(zlo, core, x, y, zhi):
    return (zlo * 2 + core, (x * 4 + y) * 2 + zhi)


class Parcel:
    def __init__(self, copy):
        self.copy, self.sent, self.received = copy, False, False

    def wait_send(self):
        if not self.sent:
            self.copy.wait_send()
        self.sent = True

    def wait_recv(self):
        if not self.received:
            self.copy.wait_recv()
        self.received = True


class Mail:
    def __init__(self, send, recv):
        self.send, self.recv = send, recv
        self.all = []

    def post(self, src, dst, target):
        copy = pltpu.make_async_remote_copy(
            src_ref=src,
            dst_ref=dst,
            send_sem=self.send.at[len(self.all)],
            recv_sem=self.recv.at[len(self.all)],
            device_id=target,
            device_id_type=pl.DeviceIdType.MESH,
        )
        copy.start()
        self.all.append(Parcel(copy))
        return self.all[-1]


def silu(v):
    return v / (1.0 + jnp.exp(-v))


def kernel(
    lat, scale, shift, fw, fbias, pw, pbias, bw, bbias, guide,
    out,
    L, G, A, FW, WZ, H, HID, WR, WP, PM, BW, CF, FR, FB, FZ, ZF, T, TS, TB, RB, OF, YB, ZB, YZ, XZ,
    HX, HY, HC, YS, CS, HZ, HZX, HZY, HZC,
    CX, CY, CC, CZ, CZX, CZY, CZC,
    lsem, ssem, rsem,
):
    zlo, core, x, y, zhi = place_of()
    mail = Mail(ssem, rsem)

    def near(sx, sy, sz):
        return device_at(zlo, core, (x + sx) % 4, (y + sy) % 4, (zhi + sz) % 2)

    def line(dz):
        z = (zhi * 4 + zlo + dz) % 8
        return device_at(z % 4, core, x, y, z // 4)

    partner = device_at(zlo, 1 - core, x, y, zhi)

    barrier = pltpu.get_barrier_semaphore()
    friends = [near(sx, sy, 0) for sx in (-1, 0, 1) for sy in (-1, 0, 1) if sx or sy]
    friends += [near(sx, sy, 1) for sx in (-1, 0, 1) for sy in (-1, 0, 1)]
    friends += [near(2, 0, 0), near(0, 2, 0)]
    friends += [line(d) for d in (1, 2, 3, 5, 6, 7)]
    friends += [partner]
    for friend in friends:
        pl.semaphore_signal(barrier, inc=1, device_id=friend, device_id_type=pl.DeviceIdType.MESH)

    loads = []

    def load(src, dst):
        copy = pltpu.make_async_copy(src, dst, lsem.at[len(loads)])
        copy.start()
        loads.append(copy)
        return copy

    load_lat = [load(lat.at[0, i * 6 : i * 6 + 6], L.at[i * 6 : i * 6 + 6]) for i in range(4)]
    load_fw = load(fw, FW)
    own_w = load(
        pw.at[:, pl.ds(pl.multiple_of(zlo * 256, 256), 256)],
        WR.at[zlo, core, x, y, pl.ds(pl.multiple_of(zhi * 32, 32), 32)],
    )
    pl.semaphore_wait(barrier, len(friends))

    rows_here = pl.ds(pl.multiple_of(zhi * 32, 32), 32)
    first = []
    for d in (4, 3, 5, 2, 6, 1, 7):
        z_there = (zhi * 4 + zlo + d) % 8 % 4
        first.append(
            mail.post(
                pw.at[:, pl.ds(pl.multiple_of(z_there * 256, 256), 256)],
                WR.at[zlo, core, x, y, rows_here],
                line(d),
            )
        )

    edge = {-1: 23, 1: 0}
    slot = {-1: 0, 1: 1}
    strip = {-1: 1, 1: 0}
    end = 11 - 11 * zhi
    fine = []
    for s in SIDES:
        fine.append(mail.post(lat.at[0, edge[s]], HX.at[slot[s]], near(-s, 0, 0)))
    half = pl.ds(pl.multiple_of(core * 12, 12), 12)
    face = mail.post(lat.at[0, half, end], HZ.at[half], near(0, 0, 1))
    above = [mail.post(lat.at[0, edge[s], end], HZX.at[slot[s]], near(-s, 0, 1)) for s in SIDES]

    gain = jnp.where(core == 1, scale[...], 1.0)
    offset = jnp.where(core == 1, shift[...], 0.0)

    def condition(values):
        return (values.astype(F32) * gain + offset).astype(BF16).astype(F32)

    def widen(i, carry):
        for z in range(12):
            at = pl.multiple_of(((z + 1) * 26 + i + 1) * 40 + 8, 8)
            G[pl.ds(at, 24), :] = condition(L[i, z])
        return carry

    for i in range(4):
        load_lat[i].wait()
        lax.fori_loop(i * 6, i * 6 + 6, widen, 0)

    def side(z, carry):
        at = ((z + 1) * 26 + 1) * 40 + 8
        YS[0, z] = G[pl.ds(at, 24, stride=40), :].astype(BF16)
        YS[1, z] = G[pl.ds(at + 23, 24, stride=40), :].astype(BF16)
        return carry

    lax.fori_loop(0, 12, side, 0)
    for sx in (0, 1):
        for sy in (0, 1):
            at = (26 + 1 + 23 * sx) * 40 + 8 + 23 * sy
            CS[sx * 2 + sy] = G[pl.ds(at, 12, stride=1040), :].astype(BF16)

    for s in SIDES:
        fine.append(mail.post(YS.at[strip[s]], HY.at[slot[s]], near(0, -s, 0)))
    for sx in SIDES:
        for sy in SIDES:
            fine.append(
                mail.post(
                    CS.at[strip[sx] * 2 + strip[sy]],
                    HC.at[slot[sx] * 2 + slot[sy]],
                    near(-sx, -sy, 0),
                )
            )
    for s in SIDES:
        above.append(mail.post(YS.at[strip[s], end], HZY.at[slot[s]], near(0, -s, 1)))
    for sx in SIDES:
        for sy in SIDES:
            above.append(
                mail.post(
                    CS.at[strip[sx] * 2 + strip[sy]],
                    HZC.at[slot[sx] * 2 + slot[sy]],
                    near(-sx, -sy, 1),
                )
            )

    load_fw.wait()
    from_ch = lax.broadcasted_iota(jnp.int32, (128, 128), 0)
    to_ch = lax.broadcasted_iota(jnp.int32, (128, 128), 1)
    group, member = to_ch >> 4, to_ch & 15
    low_ch = (member >> 2) * 16 + (member & 3) * 4 + group
    high_ch = 64 + (member >> 2) * 16 + (group - 4) * 4 + (member & 3)
    order = from_ch == jnp.where(group < 4, low_ch, high_ch)
    order16 = jnp.where(order, 1.0, 0.0).astype(BF16)

    def arrange(i, carry):
        WZ[i, 3 * 128 : 4 * 128, 0:128] = jnp.zeros((128, 128), BF16)
        WZ[i, 0:128, 128:256] = jnp.zeros((128, 128), BF16)
        for dz in range(3):
            tap = jnp.dot(FW[i * 3 + dz], order16, preferred_element_type=F32).astype(BF16)
            for o in range(2):
                at = (dz + o) * 128
                WZ[i, at : at + 128, o * 128 : o * 128 + 128] = tap
        return carry

    lax.fori_loop(0, 9, arrange, 0)
    bias = jnp.dot(
        jnp.broadcast_to(fbias[...], (8, 128)),
        jnp.where(order, 1.0, 0.0),
        preferred_element_type=F32,
        precision=lax.Precision.HIGHEST,
    )[0:1]
    bias = jnp.concatenate([bias, bias], axis=1)
    row = lax.broadcasted_iota(jnp.int32, (256, 256), 0)
    col = lax.broadcasted_iota(jnp.int32, (256, 256), 1)
    PM[...] = jnp.where(col == (row & 15) * 16 + (row >> 4), 1.0, 0.0).astype(BF16)
    H[:, 576:624, :] = jnp.zeros((4, 48, 128), F32)

    own_w.wait()
    for copy in first:
        copy.wait_recv()
    span = (slice(0, 2), slice(2, 4))
    low_x, high_y, low_y, high_x = {}, {}, {}, {}

    def low(x_at, y_at):
        return WR.at[span[0], core, x_at, y_at]

    def high(x_at, y_at):
        return WR.at[span[1], core, x_at, y_at]

    for d in (2, 1, 3):
        low_x[d] = mail.post(low(x, y), low(x, y), near(d, 0, 0))
        high_y[d] = mail.post(high(x, y), high(x, y), near(0, d, 0))
    for d in (2, 1, 3):
        low_y[0, d] = mail.post(low(x, y), low(x, y), near(0, d, 0))
        high_x[0, d] = mail.post(high(x, y), high(x, y), near(d, 0, 0))

    for copy in fine:
        copy.wait_recv()
    x_ok = (x > 0, x < 3)
    y_ok = (y > 0, y < 3)

    def border(z, carry):
        base = (z + 1) * 1040
        for s in (0, 1):
            G[pl.ds(pl.multiple_of(base + s * 1000 + 8, 8), 24), :] = jnp.where(
                x_ok[s], condition(HX[s, z]), 0.0
            )
            G[pl.ds(base + 40 + 7 + s * 25, 24, stride=40), :] = jnp.where(
                y_ok[s], HY[s, z].astype(F32), 0.0
            )
        return carry

    lax.fori_loop(0, 12, border, 0)
    for sx in (0, 1):
        for sy in (0, 1):
            G[pl.ds(1040 + sx * 1000 + 7 + sy * 25, 12, stride=1040), :] = jnp.where(
                x_ok[sx] & y_ok[sy], HC[sx * 2 + sy].astype(F32), 0.0
            )

    def fill(z):
        lanes = pl.ds(pl.multiple_of(z * 128, 128), 128)
        for parity in range(2):
            for m in range(13 - parity):
                at = z * 1040 + (2 * m + parity) * 40 + 7
                for dy in range(3):
                    pair = jnp.concatenate(
                        [G[pl.ds(at + dy, 24), :], G[pl.ds(at + dy + 40, 24), :]], axis=0
                    )
                    A[parity, dy, m * 48 : m * 48 + 48, lanes] = pair.astype(BF16)

    def inner(z, carry):
        fill(z + 1)
        return carry

    lax.fori_loop(0, 12, inner, 0)

    def conv(cz):
        for pair in range(2):
            start = pl.multiple_of((cz * 2 + pair) * 256, 256)
            total = None
            for dx in range(3):
                for dy in range(3):
                    first_row = dx // 2 * 48
                    term = jnp.dot(
                        A[dx % 2, dy, first_row : first_row + 576, pl.ds(start, 512)],
                        WZ[dx * 3 + dy],
                        preferred_element_type=F32,
                    )
                    total = term if total is None else total + term
            value = silu(total + bias)
            for i in range(24):
                at = (i % 4 * 6 + i // 4) * 24
                for o in range(2):
                    H[pair * 2 + o, at : at + 24, :] = value[
                        i * 24 : i * 24 + 24, o * 128 : o * 128 + 128
                    ]
        for zo in range(4):
            for xo in range(4):
                for yo in range(4):
                    part = xo * 16 + yo * 4 + zo
                    HID[pl.ds(pl.multiple_of(cz * 48, 16), 48), part * 128 : part * 128 + 128] = H[
                        zo, pl.ds(xo * 144 + yo, 48, stride=4), :
                    ].astype(BF16)

    for e in (1, 3, 2):
        low_x[e].wait_recv()
        x_from = (x + 4 - e) % 4
        for d in (2, 1, 3):
            low_y[e, d] = mail.post(low(x_from, y), low(x_from, y), near(0, d, 0))
        high_y[e].wait_recv()
        y_from = (y + 4 - e) % 4
        for d in (2, 1, 3):
            high_x[e, d] = mail.post(high(x, y_from), high(x, y_from), near(d, 0, 0))
    hand = {
        (0, 0): mail.post(low(slice(None), y), low(slice(None), y), partner),
        (1, 0): mail.post(high(x, slice(None)), high(x, slice(None)), partner),
    }

    own_b = [
        load(
            bw.at[:, :, pl.ds(pl.multiple_of((2 * z + core) * 128, 128), 128)],
            BW.at[:, pl.ds(pl.multiple_of(core * 128, 128), 128), z * 128 : z * 128 + 128],
        )
        for z in range(4)
    ]
    swap_b = [
        mail.post(
            bw.at[:, :, pl.ds(pl.multiple_of((2 * z + 1 - core) * 128, 128), 128)],
            BW.at[:, pl.ds(pl.multiple_of(core * 128, 128), 128), z * 128 : z * 128 + 128],
            partner,
        )
        for z in range(4)
    ]

    def far(i, carry):
        conv(i + zhi)
        return carry

    near_plane = 13 - 13 * zhi

    def blank(i, carry):
        G[pl.ds(pl.multiple_of(zrow0 + i * 40, 8), 40), :] = jnp.zeros((40, 128), F32)
        return carry

    zrow0 = (13 - near_plane) * 1040
    lax.fori_loop(0, 26, blank, 0)
    fill(13 - near_plane)
    lax.fori_loop(0, 2, far, 0)

    face.wait_recv()
    relay = mail.post(HZ.at[half], HZ.at[half], partner)
    for copy in above:
        copy.wait_recv()
    relay.wait_recv()
    base = near_plane * 1040

    def cap(i, carry):
        G[pl.ds(pl.multiple_of(base + (i + 1) * 40 + 8, 8), 24), :] = condition(HZ[i])
        return carry

    lax.fori_loop(0, 24, cap, 0)
    for s in (0, 1):
        G[pl.ds(pl.multiple_of(base + s * 1000 + 8, 8), 24), :] = jnp.where(
            x_ok[s], condition(HZX[s]), 0.0
        )
        G[pl.ds(base + 40 + 7 + s * 25, 24, stride=40), :] = jnp.where(
            y_ok[s], HZY[s].astype(F32), 0.0
        )
    for sx in (0, 1):
        for sy in (0, 1):
            there = HZC[sx * 2 + sy].astype(F32)
            cell = jnp.where(zhi == 0, there[0:1], there[11:12])
            G[pl.ds(base + sx * 1000 + 7 + sy * 25, 1), :] = jnp.where(
                x_ok[sx] & y_ok[sy], cell, 0.0
            )
    fill(near_plane)
    conv(2 - 2 * zhi)

    def regroup(upper, at):
        for part in range(4):
            block = slice(part * 16, part * 16 + 16)
            if upper:
                rows = WR[2:4, :, at, :, block, :].reshape(256, 256)
                lane = 64 + at * 16
            else:
                rows = WR[0:2, :, :, at, block, :].reshape(256, 256)
                lane = at * 16
            turned = jnp.dot(PM[...], rows, preferred_element_type=F32).astype(BF16)
            WP[block, pl.ds(pl.multiple_of(lane, 16), 16), :] = turned.reshape(16, 16, 256)

    hand[0, 0].wait_recv()
    regroup(0, y)
    hand[1, 0].wait_recv()
    regroup(1, x)
    turns = (1, 3, 2)
    for d in turns:
        for e in range(4):
            low_y[e, d].wait_recv()
        y_from = (y + 4 - d) % 4
        hand[0, d] = mail.post(low(slice(None), y_from), low(slice(None), y_from), partner)
        for e in range(4):
            high_x[e, d].wait_recv()
        x_from = (x + 4 - d) % 4
        hand[1, d] = mail.post(high(x_from, slice(None)), high(x_from, slice(None)), partner)
        if d != turns[0]:
            before = turns[turns.index(d) - 1]
            hand[0, before].wait_recv()
            regroup(0, (y + 4 - before) % 4)
            hand[1, before].wait_recv()
            regroup(1, (x + 4 - before) % 4)
    before = turns[-1]
    hand[0, before].wait_recv()
    regroup(0, (y + 4 - before) % 4)
    hand[1, before].wait_recv()
    regroup(1, (x + 4 - before) % 4)

    def project(i, total):
        lanes = pl.ds(pl.multiple_of(i * 1024, 1024), 1024)
        rows = WP[pl.ds(i * 8, 8)].reshape(1024, 256)
        return total + jnp.dot(HID[:, lanes], rows, preferred_element_type=F32)

    total = lax.fori_loop(0, 8, project, jnp.zeros((144, 256), F32))
    total = total + pbias[:, pl.ds(pl.multiple_of(zlo * 256, 256), 256)]
    total = total.astype(BF16).astype(F32)
    for h in range(2):
        CF[h] = total[:, h * 128 : h * 128 + 128]

    mine = FR.at[core]
    for cz in range(3):
        for cx in range(6):
            for h in range(2):
                mine[h, cz + 1, (cx + 1) * 8 + 1 : (cx + 1) * 8 + 7, :] = CF[
                    h, cz * 48 + cx * 6 : cz * 48 + cx * 6 + 6, :
                ]
    for cz in range(3):
        for h in range(2):
            YB[0, h, cz] = mine[h, cz + 1, pl.ds(1, 8, stride=8), :]
            YB[1, h, cz] = mine[h, cz + 1, pl.ds(6, 8, stride=8), :]
    top = 2 - 2 * zhi
    wide = {-1: 6, 1: 1}
    ZB[...] = mine[:, top + 1, 8:56].astype(BF16)
    for s in (0, 1):
        YZ[s] = YB[s, :, top].astype(BF16)
    XZ[0] = mine[:, top + 1, 8:16].astype(BF16)
    XZ[1] = mine[:, top + 1, 48:56].astype(BF16)
    around = []
    for sx in SIDES:
        for sy in SIDES:
            around.append(
                mail.post(YB.at[strip[sy]], CC.at[slot[sx] * 2 + slot[sy]], near(-sx, -sy, 0))
            )
    for s in SIDES:
        column = slice(wide[s] * 8, wide[s] * 8 + 8)
        around.append(mail.post(mine.at[:, 1:4, column], CX.at[slot[s]], near(-s, 0, 0)))
        around.append(mail.post(YB.at[strip[s]], CY.at[slot[s]], near(0, -s, 0)))
    beyond = []
    for sx in SIDES:
        for sy in SIDES:
            beyond.append(
                mail.post(YZ.at[strip[sy]], CZC.at[slot[sx] * 2 + slot[sy]], near(-sx, -sy, 1))
            )
    for s in SIDES:
        beyond.append(mail.post(XZ.at[strip[s]], CZX.at[slot[s]], near(-s, 0, 1)))
        beyond.append(mail.post(YZ.at[strip[s]], CZY.at[slot[s]], near(0, -s, 1)))
    beyond.append(mail.post(ZB, CZ, near(0, 0, 1)))
    for copy in around:
        copy.wait_send()
    for copy in around:
        copy.wait_recv()

    place8 = lax.broadcasted_iota(jnp.int32, (8, 128), 0)
    def frame(plane, in_x, in_y, in_corner):
        for s in (0, 1):
            plane[s * 56 : s * 56 + 8, :] = jnp.where(x_ok[s], in_x[s], 0.0)
        for s in (0, 1):
            low_row = jnp.broadcast_to(in_corner[s][6:7], (8, 128))
            high_row = jnp.broadcast_to(in_corner[2 + s][1:2], (8, 128))
            value = jnp.where(place8 == 0, jnp.where(x_ok[0], low_row, 0.0), in_y[s])
            value = jnp.where(place8 == 7, jnp.where(x_ok[1], high_row, 0.0), value)
            plane[pl.ds(s * 7, 8, stride=8), :] = jnp.where(y_ok[s], value, 0.0)

    for h in range(2):
        for cz in range(3):
            frame(
                mine.at[h, cz + 1],
                [CX[s, h, cz] for s in (0, 1)],
                [CY[s, h, cz] for s in (0, 1)],
                [CC[s, h, cz] for s in range(4)],
            )
    trade = mail.post(mine.at[:, 1:4], mine.at[:, 1:4], partner)

    def spread(w, put):
        for dy in range(3):
            turned = w if dy == 0 else pltpu.roll(w, 64 - dy, 0)
            for dx in range(3):
                put(dx * 3 + dy, turned[dx * 8 : dx * 8 + 48].astype(BF16))

    def lay(c, z, h):
        def put(i, rows):
            FB[i, c, z, :, h * 128 : h * 128 + 128] = rows

        spread(FR[c, h, z], put)

    def blank_ends(i, carry):
        for c in range(2):
            for z in (0, 4):
                FB[i, c, z] = jnp.zeros((48, 256), BF16)
        return carry

    lax.fori_loop(0, 9, blank_ends, 0)

    def stack_own(i, carry):
        for h in range(2):
            lay(core, i + 1, h)
        return carry

    lax.fori_loop(0, 3, stack_own, 0)
    trade.wait_recv()

    def stack_other(i, carry):
        for h in range(2):
            lay(1 - core, i + 1, h)
        return carry

    lax.fori_loop(0, 3, stack_other, 0)

    for copy in own_b:
        copy.wait()
    for copy in swap_b:
        copy.wait_recv()
    first_half = 1 - zlo // 2

    def bottle(step, carry):
        n = pl.ds(pl.multiple_of(((first_half + step) % 2) * 256, 256), 256)
        T[step] = jnp.zeros((288, 256), F32)

        def taps(i, carry):
            total = T[step]
            for dz in range(3):
                rows = FB[i, :, dz : dz + 3].reshape(288, 256)
                total = total + jnp.dot(rows, BW[i * 3 + dz, :, n], preferred_element_type=F32)
            T[step] = total
            return carry

        return lax.fori_loop(0, 9, taps, carry)

    lax.fori_loop(0, 2, bottle, 0)

    for copy in beyond:
        copy.wait_recv()
    for h in range(2):
        ZF[core, h, 8:56, :] = CZ[h].astype(F32)
        frame(
            ZF.at[core, h],
            [CZX[s, h].astype(F32) for s in (0, 1)],
            [CZY[s, h].astype(F32) for s in (0, 1)],
            [CZC[s, h].astype(F32) for s in range(4)],
        )
    trade_z = mail.post(ZF.at[core], ZF.at[core], partner)
    trade_z.wait_recv()
    for c in range(2):
        for h in range(2):

            def put(i, rows, c=c, h=h):
                FZ[i, c * 48 : c * 48 + 48, h * 128 : h * 128 + 128] = rows

            spread(ZF[c, h], put)

    gather = []
    for step in range(2):
        half_at = (first_half + step) % 2
        n = pl.ds(pl.multiple_of(half_at * 256, 256), 256)

        def cap_taps(i, total):
            return total + jnp.dot(FZ[i], BW[i * 3 + top, :, n], preferred_element_type=F32)

        extra = lax.fori_loop(0, 9, cap_taps, jnp.zeros((96, 256), F32))
        for c in range(2):
            at = pl.ds(pl.multiple_of(c * 144 + top * 48, 16), 48)
            T[step, at, :] = T[step, at, :] + extra[c * 48 : c * 48 + 48]
        for c in range(2):
            for g in range(18):
                at = (c * 18 + g) * 8
                for j in range(2):
                    TS[half_at * 2 + j, c, g * 6 : g * 6 + 6, :] = T[
                        step, at : at + 6, j * 128 : j * 128 + 128
                    ]
        if step == 0:
            targets = [half_at * 2 + (zlo + j) % 2 for j in range(2)]
        else:
            targets = [half_at * 2 + (zlo + 1) % 2]
        for z in targets:
            TB[len(gather)] = TS[z].astype(TB.dtype)
            gather.append(
                mail.post(
                    TB.at[len(gather)], RB.at[len(gather)], device_at(z, core, x, y, zhi)
                )
            )
    for copy in gather:
        copy.wait_recv()
    lane = pl.ds(pl.multiple_of((zlo * 2 + core) * 128, 128), 128)
    result = []
    for c in range(2):
        value = TS[zlo, c]
        for j in range(3):
            value = value + RB[j, c].astype(F32)
        result.append(silu(value + bbias[:, lane]))
    OF[...] = result[0] + guide[0] * (result[1] - result[0])
    for g in range(18):
        out[g // 6, g % 6, 0:6, :] = OF[g * 6 : g * 6 + 6, :].astype(BF16)
    for g in range(18):
        out[g // 6, g % 6, 6:8, :] = jnp.zeros((2, 128), BF16)

    for copy in mail.all:
        copy.wait_send()


MESSAGES = 120


def shards(lat, scale, shift, fw, fbias, pw, pbias, bw, bbias, guide):
    anywhere = pl.BlockSpec(memory_space=pl.ANY)
    vmem = pl.BlockSpec(memory_space=pltpu.VMEM)
    scratch = [
        pltpu.VMEM((24, 12, 24, 128), BF16),
        pltpu.VMEM((14 * 1040, 128), F32),
        pltpu.VMEM((2, 3, 624, 14 * 128), BF16),
        pltpu.VMEM((27, 128, 128), BF16),
        pltpu.VMEM((9, 512, 256), BF16),
        pltpu.VMEM((4, 624, 128), F32),
        pltpu.VMEM((144, 8192), BF16),
        pltpu.VMEM((4, 2, 4, 4, 64, 256), BF16),
        pltpu.VMEM((64, 128, 256), BF16),
        pltpu.VMEM((256, 256), BF16),
        pltpu.VMEM((27, 256, 512), BF16),
        pltpu.VMEM((2, 144, 128), F32),
        pltpu.VMEM((2, 2, 5, 64, 128), F32),
        pltpu.VMEM((9, 2, 5, 48, 256), BF16),
        pltpu.VMEM((9, 96, 256), BF16),
        pltpu.VMEM((2, 2, 64, 128), F32),
        pltpu.VMEM((2, 288, 256), F32),
        pltpu.VMEM((4, 2, 108, 128), F32),
        pltpu.VMEM((3, 2, 108, 128), BF16),
        pltpu.VMEM((3, 2, 108, 128), BF16),
        pltpu.VMEM((108, 128), F32),
        pltpu.VMEM((2, 2, 3, 8, 128), F32),
        pltpu.VMEM((2, 48, 128), BF16),
        pltpu.VMEM((2, 2, 8, 128), BF16),
        pltpu.VMEM((2, 2, 8, 128), BF16),
        pltpu.VMEM((2, 12, 24, 128), BF16),
        pltpu.VMEM((2, 12, 24, 128), BF16),
        pltpu.VMEM((4, 12, 128), BF16),
        pltpu.VMEM((2, 12, 24, 128), BF16),
        pltpu.VMEM((4, 12, 128), BF16),
        pltpu.VMEM((24, 24, 128), BF16),
        pltpu.VMEM((2, 24, 128), BF16),
        pltpu.VMEM((2, 24, 128), BF16),
        pltpu.VMEM((4, 12, 128), BF16),
        pltpu.VMEM((2, 2, 3, 8, 128), F32),
        pltpu.VMEM((2, 2, 3, 8, 128), F32),
        pltpu.VMEM((4, 2, 3, 8, 128), F32),
        pltpu.VMEM((2, 48, 128), BF16),
        pltpu.VMEM((2, 2, 8, 128), BF16),
        pltpu.VMEM((2, 2, 8, 128), BF16),
        pltpu.VMEM((4, 2, 8, 128), BF16),
        pltpu.SemaphoreType.DMA((16,)),
        pltpu.SemaphoreType.DMA((MESSAGES,)),
        pltpu.SemaphoreType.DMA((MESSAGES,)),
    ]
    rows = pl.pallas_call(
        kernel,
        out_shape=jax.ShapeDtypeStruct((3, 6, 8, 128), BF16),
        in_specs=[
            anywhere, vmem, vmem, anywhere, vmem, anywhere, vmem, anywhere, vmem,
            pl.BlockSpec(memory_space=pltpu.SMEM),
        ],
        out_specs=vmem,
        scratch_shapes=scratch,
        compiler_params=pltpu.CompilerParams(
            collective_id=0, has_side_effects=True, vmem_limit_bytes=67043328
        ),
        name="denoise",
    )(
        lat.transpose(0, 1, 3, 2, 4),
        scale.reshape(1, -1),
        shift.reshape(1, -1),
        fw.reshape(27, 128, 128),
        fbias.reshape(1, -1),
        pw,
        pbias.reshape(1, -1),
        bw,
        bbias.reshape(1, -1),
        guide,
    )
    return rows[:, :, :6].transpose(1, 2, 0, 3)[None]


def solution(mesh):
    placed = (
        P("region", None, None, None, None),
        P(),
        P(),
        P(),
        P(),
        P(("chan", "region"), None),
        P(),
        P(None, "chan", None),
        P(),
        P(),
    )
    return jax.shard_map(
        shards,
        mesh=mesh,
        in_specs=placed,
        out_specs=P("region", None, None, None, "chan"),
        check_vma=False,
    )
```

time: 860 us -> 70.1 us (0.08)
  waiting for transfers between devices: 660 us -> 0 us
  local copies, waits for them, and re-layouts: 94.6 us -> 1.4 us
  Pallas kernels: 0 us -> 67.9 us
  starting transfers between devices: 41.1 us -> 0 us
  matrix products: 22.2 us -> 0 us
  blocking collectives: 15.1 us -> 0 us
  between operations: 15.2 us -> 0.66 us
    all_gather x1 -> x0, waiting for transfers between devices: 593 us -> none  [shards(): lax.all_gather(proj_weight, ('chan', 'region'), axis=0, tiled=True)]
    pallas_call x0 -> x1, Pallas kernels: none -> 67.9 us  [shards(): pl.pallas_call(kernel, out_shape=jax.ShapeDtypeStruct((3, 6, 8, 128), BF1...]
    another operation x2 -> x0, local copies, waits for them, and re-layouts: 54.6 us -> none  [the longest x1 37.1 us: shards(): flat = patches.reshape(tiles_dev * cells ** 3, depth)]
    ppermute x12 -> x0, starting transfers between devices: 41.1 us -> none  [passed_along(): lax.ppermute(value, axis, [(source, source + steps) for source in range(l...]
    reduce_scatter x1 -> x0, waiting for transfers between devices: 35.1 us -> none  [shards(): summed = lax.psum_scatter(terms, 'chan', scatter_dimension=1, tiled=True)]
    ppermute x12 -> x0, waiting for transfers between devices: 31.4 us -> none  [passed_along(): lax.ppermute(value, axis, [(source, source + steps) for source in range(l...]
    dot_general x3 -> x0, matrix products: 22.2 us -> none  [the longest x1 8.75 us: shards(): jnp.dot(flat, lax.all_gather(proj_weight, ('chan', 'region'), axis=0, til...]
    reshape x1 -> x0, local copies, waits for them, and re-layouts: 18.7 us -> none  [fine_conv(): stacked = stacked.reshape(side ** 3, -1)]
  transfers between devices with their start and end apart: 14 -> 0, of which waited for: 11 -> 0; matrix products, arithmetic and copies ran while one was open for 12% -> 0% of each run, Pallas kernels for 0% -> 0%
where the time goes in v2:
time: 70.1 us; the launch traced here: 70 us
  Pallas kernels  67.9 us (97%)
  local copies, waits for them, and re-layouts  1.4 us (2%)
    pallas_call x1, Pallas kernels, shards(): pl.pallas_call(kernel, out_shape=jax.ShapeDtypeStruct((3, 6, 8, 128), BF1...  67.9 us
    broadcast_in_dim x2, local copies, waits for them, and re-layouts, shards(): return rows[:, :, :6].transpose(1, 2, 0, 3)[None]  1.4 us

profile of v2, /device:TPU:1, one launch (start us, length us, event | category | flops | bytes accessed | tf_op | source)
XLA Modules:
  0.0 70.0 jit_solution(178635647715982064)
XLA Ops:
  0.7 67.9 %denoise.1 = bf16[3,6,8,128]{3,2,1,0:T(8,128)(2,1)} custom-call(bf16[1,24,12,24,128]{4,3,2,1,0:T(8,128)(2,1)} %bitcast.11, f32[1,128]{1,0:T(1,128)} %bitcast.15, f32[1,128]{1,0:T(1,128)} %bitcast.16, bf16[27,128,128]{2,1,0:T(8,128)(2,1)} %bitcast.12, f32[1,128]{1,0:T(1,128)} %bitcast.17, bf16[32,1024]{1,0:T(8,128)(2,1)} %pw.1, f32[1,1024]{1,0:T(1,128)} %bitcast.13, ...), custom_call_target="tpu_custom_call" | custom-call | tf_op jit(solution)/shard_map/denoise/pallas_call | solution.py:666
  68.6 0.8 %slice_bitcast_fusion = bf16[1,6,6,3,128]{4,2,1,3,0:T(8,128)(2,1)S(1)} fusion(bf16[3,6,8,128]{3,2,1,0:T(8,128)(2,1)} %denoise.1), kind=kLoop, calls=%fused_computation | loop fusion | bytes 55296 | tf_op jit(solution)/shard_map/broadcast_in_dim | solution.py:691
  69.3 0.6 copy.11

commit v3 on v2

--- a/solution.py
+++ b/solution.py
@@ -124,9 +124,6 @@
     fine = []
     for s in SIDES:
         fine.append(mail.post(lat.at[0, edge[s]], HX.at[slot[s]], near(-s, 0, 0)))
-    half = pl.ds(pl.multiple_of(core * 12, 12), 12)
-    face = mail.post(lat.at[0, half, end], HZ.at[half], near(0, 0, 1))
-    above = [mail.post(lat.at[0, edge[s], end], HZX.at[slot[s]], near(-s, 0, 1)) for s in SIDES]
 
     gain = jnp.where(core == 1, scale[...], 1.0)
     offset = jnp.where(core == 1, shift[...], 0.0)
@@ -167,18 +164,6 @@
                     near(-sx, -sy, 0),
                 )
             )
-    for s in SIDES:
-        above.append(mail.post(YS.at[strip[s], end], HZY.at[slot[s]], near(0, -s, 1)))
-    for sx in SIDES:
-        for sy in SIDES:
-            above.append(
-                mail.post(
-                    CS.at[strip[sx] * 2 + strip[sy]],
-                    HZC.at[slot[sx] * 2 + slot[sy]],
-                    near(-sx, -sy, 1),
-                )
-            )
-
     load_fw.wait()
     from_ch = lax.broadcasted_iota(jnp.int32, (128, 128), 0)
     to_ch = lax.broadcasted_iota(jnp.int32, (128, 128), 1)
@@ -214,21 +199,101 @@
     own_w.wait()
     for copy in first:
         copy.wait_recv()
-    span = (slice(0, 2), slice(2, 4))
-    low_x, high_y, low_y, high_x = {}, {}, {}, {}
-
-    def low(x_at, y_at):
-        return WR.at[span[0], core, x_at, y_at]
-
-    def high(x_at, y_at):
-        return WR.at[span[1], core, x_at, y_at]
-
-    for d in (2, 1, 3):
-        low_x[d] = mail.post(low(x, y), low(x, y), near(d, 0, 0))
-        high_y[d] = mail.post(high(x, y), high(x, y), near(0, d, 0))
-    for d in (2, 1, 3):
-        low_y[0, d] = mail.post(low(x, y), low(x, y), near(0, d, 0))
-        high_x[0, d] = mail.post(high(x, y), high(x, y), near(d, 0, 0))
+
+    def low(j, x_at, y_at):
+        return WR.at[j, core, x_at % 4, y_at % 4]
+
+    def high(j, x_at, y_at):
+        return low(j, x_at, y_at)
+
+    both = {"low": slice(0, 2), "high": slice(2, 4)}
+    base_of = {"low": 0, "high": 2}
+
+    class Ring:
+        def __init__(self, part, along_x, shift):
+            self.part, self.along_x, self.shift = part, along_x, shift
+            block = self.at(both[part], 0)
+            self.up = mail.post(block, block, self.to(1))
+            self.down = mail.post(block, block, self.to(-1))
+
+        def at(self, j, step):
+            if self.along_x:
+                return low(j, x + 4 + step, y + 4 + self.shift)
+            return low(j, x + 4 + self.shift, y + 4 + step)
+
+        def to(self, step):
+            return near(4 + step, 0, 0) if self.along_x else near(0, 4 + step, 0)
+
+        def relay(self):
+            self.up.wait_recv()
+            piece = self.at(base_of[self.part], -1)
+            self.up2 = mail.post(piece, piece, self.to(1))
+            self.down.wait_recv()
+            piece = self.at(base_of[self.part] + 1, 1)
+            self.down2 = mail.post(piece, piece, self.to(-1))
+
+        def finish(self):
+            self.up2.wait_recv()
+            self.down2.wait_recv()
+
+    low_x = Ring("low", True, 0)
+    high_y = Ring("high", False, 0)
+    low_y = {0: Ring("low", False, 0)}
+    high_x = {0: Ring("high", True, 0)}
+
+    half = pl.ds(pl.multiple_of(core * 12, 12), 12)
+    face = mail.post(lat.at[0, half, end], HZ.at[half], near(0, 0, 1))
+    above = [mail.post(lat.at[0, edge[s], end], HZX.at[slot[s]], near(-s, 0, 1)) for s in SIDES]
+    for s in SIDES:
+        above.append(mail.post(YS.at[strip[s], end], HZY.at[slot[s]], near(0, -s, 1)))
+    for sx in SIDES:
+        for sy in SIDES:
+            above.append(
+                mail.post(
+                    CS.at[strip[sx] * 2 + strip[sy]],
+                    HZC.at[slot[sx] * 2 + slot[sy]],
+                    near(-sx, -sy, 1),
+                )
+            )
+
+    def step_one():
+        low_x.relay()
+        high_y.relay()
+        for e in (-1, 1):
+            low_y[e] = Ring("low", False, e)
+            high_x[e] = Ring("high", True, e)
+        low_y[0].relay()
+        high_x[0].relay()
+
+    def step_two():
+        low_x.finish()
+        high_y.finish()
+        low_y[2] = Ring("low", False, 2)
+        high_x[2] = Ring("high", True, 2)
+
+    hand = {}
+
+    def pass_low(step):
+        column = WR.at[both["low"], core, :, (y + 4 + step) % 4]
+        hand["low", step] = mail.post(column, column, partner)
+
+    def pass_high(step):
+        column = WR.at[both["high"], core, (x + 4 + step) % 4]
+        hand["high", step] = mail.post(column, column, partner)
+
+    def step_three():
+        pass_low(0)
+        pass_high(0)
+        for e in (-1, 1):
+            low_y[e].relay()
+            high_x[e].relay()
+
+    def step_four():
+        low_y[2].relay()
+        high_x[2].relay()
+        for e in (-1, 1):
+            pass_low(e)
+            pass_high(e)
 
     for copy in fine:
         copy.wait_recv()
@@ -270,26 +335,27 @@
 
     lax.fori_loop(0, 12, inner, 0)
 
-    def conv(cz):
-        for pair in range(2):
-            start = pl.multiple_of((cz * 2 + pair) * 256, 256)
-            total = None
-            for dx in range(3):
-                for dy in range(3):
-                    first_row = dx // 2 * 48
-                    term = jnp.dot(
-                        A[dx % 2, dy, first_row : first_row + 576, pl.ds(start, 512)],
-                        WZ[dx * 3 + dy],
-                        preferred_element_type=F32,
-                    )
-                    total = term if total is None else total + term
-            value = silu(total + bias)
-            for i in range(24):
-                at = (i % 4 * 6 + i // 4) * 24
-                for o in range(2):
-                    H[pair * 2 + o, at : at + 24, :] = value[
-                        i * 24 : i * 24 + 24, o * 128 : o * 128 + 128
-                    ]
+    def conv(cz, pair):
+        start = pl.multiple_of((cz * 2 + pair) * 256, 256)
+        total = None
+        for dx in range(3):
+            for dy in range(3):
+                first_row = dx // 2 * 48
+                term = jnp.dot(
+                    A[dx % 2, dy, first_row : first_row + 576, pl.ds(start, 512)],
+                    WZ[dx * 3 + dy],
+                    preferred_element_type=F32,
+                )
+                total = term if total is None else total + term
+        value = silu(total + bias)
+        for i in range(24):
+            at = (i % 4 * 6 + i // 4) * 24
+            for o in range(2):
+                H[pair * 2 + o, at : at + 24, :] = value[
+                    i * 24 : i * 24 + 24, o * 128 : o * 128 + 128
+                ]
+
+    def collect(cz):
         for zo in range(4):
             for xo in range(4):
                 for yo in range(4):
@@ -298,19 +364,7 @@
                         zo, pl.ds(xo * 144 + yo, 48, stride=4), :
                     ].astype(BF16)
 
-    for e in (1, 3, 2):
-        low_x[e].wait_recv()
-        x_from = (x + 4 - e) % 4
-        for d in (2, 1, 3):
-            low_y[e, d] = mail.post(low(x_from, y), low(x_from, y), near(0, d, 0))
-        high_y[e].wait_recv()
-        y_from = (y + 4 - e) % 4
-        for d in (2, 1, 3):
-            high_x[e, d] = mail.post(high(x, y_from), high(x, y_from), near(d, 0, 0))
-    hand = {
-        (0, 0): mail.post(low(slice(None), y), low(slice(None), y), partner),
-        (1, 0): mail.post(high(x, slice(None)), high(x, slice(None)), partner),
-    }
+    step_one()
 
     own_b = [
         load(
@@ -328,10 +382,6 @@
         for z in range(4)
     ]
 
-    def far(i, carry):
-        conv(i + zhi)
-        return carry
-
     near_plane = 13 - 13 * zhi
 
     def blank(i, carry):
@@ -341,10 +391,17 @@
     zrow0 = (13 - near_plane) * 1040
     lax.fori_loop(0, 26, blank, 0)
     fill(13 - near_plane)
-    lax.fori_loop(0, 2, far, 0)
-
+    conv(zhi, 0)
+    step_two()
+    conv(zhi, 1)
+    collect(zhi)
     face.wait_recv()
     relay = mail.post(HZ.at[half], HZ.at[half], partner)
+    step_three()
+    conv(zhi + 1, 0)
+    step_four()
+    conv(zhi + 1, 1)
+    collect(zhi + 1)
     for copy in above:
         copy.wait_recv()
     relay.wait_recv()
@@ -370,7 +427,9 @@
                 x_ok[sx] & y_ok[sy], cell, 0.0
             )
     fill(near_plane)
-    conv(2 - 2 * zhi)
+    conv(2 - 2 * zhi, 0)
+    conv(2 - 2 * zhi, 1)
+    collect(2 - 2 * zhi)
 
     def regroup(upper, at):
         for part in range(4):
@@ -384,31 +443,17 @@
             turned = jnp.dot(PM[...], rows, preferred_element_type=F32).astype(BF16)
             WP[block, pl.ds(pl.multiple_of(lane, 16), 16), :] = turned.reshape(16, 16, 256)
 
-    hand[0, 0].wait_recv()
-    regroup(0, y)
-    hand[1, 0].wait_recv()
-    regroup(1, x)
-    turns = (1, 3, 2)
-    for d in turns:
-        for e in range(4):
-            low_y[e, d].wait_recv()
-        y_from = (y + 4 - d) % 4
-        hand[0, d] = mail.post(low(slice(None), y_from), low(slice(None), y_from), partner)
-        for e in range(4):
-            high_x[e, d].wait_recv()
-        x_from = (x + 4 - d) % 4
-        hand[1, d] = mail.post(high(x_from, slice(None)), high(x_from, slice(None)), partner)
-        if d != turns[0]:
-            before = turns[turns.index(d) - 1]
-            hand[0, before].wait_recv()
-            regroup(0, (y + 4 - before) % 4)
-            hand[1, before].wait_recv()
-            regroup(1, (x + 4 - before) % 4)
-    before = turns[-1]
-    hand[0, before].wait_recv()
-    regroup(0, (y + 4 - before) % 4)
-    hand[1, before].wait_recv()
-    regroup(1, (x + 4 - before) % 4)
+    for ring in (low_y[-1], low_y[1], low_y[0], low_y[2]):
+        ring.finish()
+    pass_low(2)
+    for ring in (high_x[-1], high_x[1], high_x[0], high_x[2]):
+        ring.finish()
+    pass_high(2)
+    for step in (0, -1, 1, 2):
+        hand["low", step].wait_recv()
+        regroup(0, (y + 4 + step) % 4)
+        hand["high", step].wait_recv()
+        regroup(1, (x + 4 + step) % 4)
 
     def project(i, total):
         lanes = pl.ds(pl.multiple_of(i * 1024, 1024), 1024)
@@ -526,8 +571,11 @@
         copy.wait_recv()
     first_half = 1 - zlo // 2
 
-    def bottle(step, carry):
-        n = pl.ds(pl.multiple_of(((first_half + step) % 2) * 256, 256), 256)
+    def columns(step):
+        return pl.ds(pl.multiple_of(((first_half + step) % 2) * 256, 256), 256)
+
+    def bottle(step):
+        n = columns(step)
         T[step] = jnp.zeros((288, 256), F32)
 
         def taps(i, carry):
@@ -538,9 +586,42 @@
             T[step] = total
             return carry
 
-        return lax.fori_loop(0, 9, taps, carry)
-
-    lax.fori_loop(0, 2, bottle, 0)
+        lax.fori_loop(0, 9, taps, 0)
+
+    def compact(step, cz):
+        at = (first_half + step) % 2 * 2
+        for c in range(2):
+            for cx in range(6):
+                row = pl.multiple_of(c * 144 + cz * 48 + cx * 8, 8)
+                for j in range(2):
+                    TS[at + j, cz, c, cx * 6 : cx * 6 + 6, :] = T[
+                        step, pl.ds(row, 6), j * 128 : j * 128 + 128
+                    ]
+
+    across = [(first_half % 2) * 2 + (zlo + j) % 2 for j in range(2)]
+    across.append((first_half + 1) % 2 * 2 + (zlo + 1) % 2)
+    gather = []
+
+    def ship(m, layers, static):
+        for cz in static:
+            for c in range(2):
+                TB[m, cz, c] = TS[across[m], cz, c].astype(BF16)
+        gather.append(
+            mail.post(
+                TB.at[m, layers], RB.at[m, layers], device_at(across[m], core, x, y, zhi)
+            )
+        )
+
+    ready = pl.ds(zhi, 2)
+    bottle(0)
+    for cz in range(2):
+        compact(0, zhi + cz)
+    for m in (0, 1):
+        ship(m, ready, (zhi, zhi + 1))
+    bottle(1)
+    for cz in range(2):
+        compact(1, zhi + cz)
+    ship(2, ready, (zhi, zhi + 1))
 
     for copy in beyond:
         copy.wait_recv()
@@ -562,10 +643,8 @@
 
             spread(ZF[c, h], put)
 
-    gather = []
     for step in range(2):
-        half_at = (first_half + step) % 2
-        n = pl.ds(pl.multiple_of(half_at * 256, 256), 256)
+        n = columns(step)
 
         def cap_taps(i, total):
             return total + jnp.dot(FZ[i], BW[i * 3 + top, :, n], preferred_element_type=F32)
@@ -574,38 +653,23 @@
         for c in range(2):
             at = pl.ds(pl.multiple_of(c * 144 + top * 48, 16), 48)
             T[step, at, :] = T[step, at, :] + extra[c * 48 : c * 48 + 48]
-        for c in range(2):
-            for g in range(18):
-                at = (c * 18 + g) * 8
-                for j in range(2):
-                    TS[half_at * 2 + j, c, g * 6 : g * 6 + 6, :] = T[
-                        step, at : at + 6, j * 128 : j * 128 + 128
-                    ]
-        if step == 0:
-            targets = [half_at * 2 + (zlo + j) % 2 for j in range(2)]
-        else:
-            targets = [half_at * 2 + (zlo + 1) % 2]
-        for z in targets:
-            TB[len(gather)] = TS[z].astype(TB.dtype)
-            gather.append(
-                mail.post(
-                    TB.at[len(gather)], RB.at[len(gather)], device_at(z, core, x, y, zhi)
-                )
-            )
+        compact(step, top)
+        for m in ((0, 1), (2,))[step]:
+            ship(m, top, (top,))
     for copy in gather:
         copy.wait_recv()
     lane = pl.ds(pl.multiple_of((zlo * 2 + core) * 128, 128), 128)
-    result = []
-    for c in range(2):
-        value = TS[zlo, c]
-        for j in range(3):
-            value = value + RB[j, c].astype(F32)
-        result.append(silu(value + bbias[:, lane]))
-    OF[...] = result[0] + guide[0] * (result[1] - result[0])
-    for g in range(18):
-        out[g // 6, g % 6, 0:6, :] = OF[g * 6 : g * 6 + 6, :].astype(BF16)
-    for g in range(18):
-        out[g // 6, g % 6, 6:8, :] = jnp.zeros((2, 128), BF16)
+    for cz in range(3):
+        result = []
+        for c in range(2):
+            value = TS[zlo, cz, c]
+            for j in range(3):
+                value = value + RB[j, cz, c].astype(F32)
+            result.append(silu(value + bbias[:, lane]))
+        OF[...] = result[0] + guide[0] * (result[1] - result[0])
+        for cx in range(6):
+            out[cz, cx, 0:6, :] = OF[cx * 6 : cx * 6 + 6, :].astype(BF16)
+            out[cz, cx, 6:8, :] = jnp.zeros((2, 128), BF16)
 
     for copy in mail.all:
         copy.wait_send()
@@ -635,10 +699,10 @@
         pltpu.VMEM((9, 96, 256), BF16),
         pltpu.VMEM((2, 2, 64, 128), F32),
         pltpu.VMEM((2, 288, 256), F32),
-        pltpu.VMEM((4, 2, 108, 128), F32),
-        pltpu.VMEM((3, 2, 108, 128), BF16),
-        pltpu.VMEM((3, 2, 108, 128), BF16),
-        pltpu.VMEM((108, 128), F32),
+        pltpu.VMEM((4, 3, 2, 36, 128), F32),
+        pltpu.VMEM((3, 3, 2, 36, 128), BF16),
+        pltpu.VMEM((3, 3, 2, 36, 128), BF16),
+        pltpu.VMEM((36, 128), F32),
         pltpu.VMEM((2, 2, 3, 8, 128), F32),
         pltpu.VMEM((2, 48, 128), BF16),
         pltpu.VMEM((2, 2, 8, 128), BF16),

time: 70.1 us -> 65.1 us (0.929)
  Pallas kernels: 67.9 us -> 62.5 us
    pallas_call x1, Pallas kernels: 67.9 us -> 62.5 us  [shards(): pl.pallas_call(kernel, out_shape=jax.ShapeDtypeStruct((3, 6, 8, 128), BF1...]
where the time goes in v3:
time: 65.1 us; the launch traced here: 64.5 us
  Pallas kernels  62.5 us (96%)
  local copies, waits for them, and re-layouts  1.4 us (2%)
  between operations  0.66 us (1%)
    pallas_call x1, Pallas kernels, shards(): pl.pallas_call(kernel, out_shape=jax.ShapeDtypeStruct((3, 6, 8, 128), BF1...  62.5 us
    broadcast_in_dim x2, local copies, waits for them, and re-layouts, shards(): return rows[:, :, :6].transpose(1, 2, 0, 3)[None]  1.4 us

profile of v3, /device:TPU:1, one launch (start us, length us, event | category | flops | bytes accessed | tf_op | source)
XLA Modules:
  0.0 64.5 jit_solution(5746253551848605531)
XLA Ops:
  0.7 62.5 %denoise.1 = bf16[3,6,8,128]{3,2,1,0:T(8,128)(2,1)} custom-call(bf16[1,24,12,24,128]{4,3,2,1,0:T(8,128)(2,1)} %bitcast.11, f32[1,128]{1,0:T(1,128)} %bitcast.15, f32[1,128]{1,0:T(1,128)} %bitcast.16, bf16[27,128,128]{2,1,0:T(8,128)(2,1)} %bitcast.12, f32[1,128]{1,0:T(1,128)} %bitcast.17, bf16[32,1024]{1,0:T(8,128)(2,1)} %pw.1, f32[1,1024]{1,0:T(1,128)} %bitcast.13, ...), custom_call_target="tpu_custom_call" | custom-call | tf_op jit(solution)/shard_map/denoise/pallas_call | solution.py:730
  63.1 0.8 %slice_bitcast_fusion = bf16[1,6,6,3,128]{4,2,1,3,0:T(8,128)(2,1)S(1)} fusion(bf16[3,6,8,128]{3,2,1,0:T(8,128)(2,1)} %denoise.1), kind=kLoop, calls=%fused_computation | loop fusion | bytes 55296 | tf_op jit(solution)/shard_map/broadcast_in_dim | solution.py:755
  63.9 0.6 copy.11

commit v4 on v3

--- a/solution.py
+++ b/solution.py
@@ -443,17 +443,21 @@
             turned = jnp.dot(PM[...], rows, preferred_element_type=F32).astype(BF16)
             WP[block, pl.ds(pl.multiple_of(lane, 16), 16), :] = turned.reshape(16, 16, 256)
 
+    def regroup_from(step):
+        hand["low", step].wait_recv()
+        regroup(0, (y + 4 + step) % 4)
+        hand["high", step].wait_recv()
+        regroup(1, (x + 4 + step) % 4)
+
+    for step in (0, -1, 1):
+        regroup_from(step)
     for ring in (low_y[-1], low_y[1], low_y[0], low_y[2]):
         ring.finish()
     pass_low(2)
     for ring in (high_x[-1], high_x[1], high_x[0], high_x[2]):
         ring.finish()
     pass_high(2)
-    for step in (0, -1, 1, 2):
-        hand["low", step].wait_recv()
-        regroup(0, (y + 4 + step) % 4)
-        hand["high", step].wait_recv()
-        regroup(1, (x + 4 + step) % 4)
+    regroup_from(2)
 
     def project(i, total):
         lanes = pl.ds(pl.multiple_of(i * 1024, 1024), 1024)

time: 65.1 us -> 66.6 us (1.023)
  Pallas kernels: 62.5 us -> 64.4 us
    pallas_call x1, Pallas kernels: 62.5 us -> 64.4 us  [shards(): pl.pallas_call(kernel, out_shape=jax.ShapeDtypeStruct((3, 6, 8, 128), BF1...]
where the time goes in v4:
time: 66.6 us; the launch traced here: 66.4 us
  Pallas kernels  64.4 us (97%)
  local copies, waits for them, and re-layouts  1.4 us (2%)
    pallas_call x1, Pallas kernels, shards(): pl.pallas_call(kernel, out_shape=jax.ShapeDtypeStruct((3, 6, 8, 128), BF1...  64.4 us
    broadcast_in_dim x2, local copies, waits for them, and re-layouts, shards(): return rows[:, :, :6].transpose(1, 2, 0, 3)[None]  1.4 us

profile of v4, /device:TPU:1, one launch (start us, length us, event | category | flops | bytes accessed | tf_op | source)
XLA Modules:
  0.0 66.4 jit_solution(7169027755592992036)
XLA Ops:
  0.7 64.4 %denoise.1 = bf16[3,6,8,128]{3,2,1,0:T(8,128)(2,1)} custom-call(bf16[1,24,12,24,128]{4,3,2,1,0:T(8,128)(2,1)} %bitcast.11, f32[1,128]{1,0:T(1,128)} %bitcast.15, f32[1,128]{1,0:T(1,128)} %bitcast.16, bf16[27,128,128]{2,1,0:T(8,128)(2,1)} %bitcast.12, f32[1,128]{1,0:T(1,128)} %bitcast.17, bf16[32,1024]{1,0:T(8,128)(2,1)} %pw.1, f32[1,1024]{1,0:T(1,128)} %bitcast.13, ...), custom_call_target="tpu_custom_call" | custom-call | tf_op jit(solution)/shard_map/denoise/pallas_call | solution.py:734
  65.0 0.8 %slice_bitcast_fusion = bf16[1,6,6,3,128]{4,2,1,3,0:T(8,128)(2,1)S(1)} fusion(bf16[3,6,8,128]{3,2,1,0:T(8,128)(2,1)} %denoise.1), kind=kLoop, calls=%fused_computation | loop fusion | bytes 55296 | tf_op jit(solution)/shard_map/broadcast_in_dim | solution.py:759
  65.8 0.6 copy.11
